TPU v7x, 32 devices: a whole 2x2x4 slice. The times are simulated.
32 devices in a mesh: fsdp: 8 (over z, y), dp: 4 (over x, core).
Axes of the slice: x: 2, y: 2, z: 4, core: 2. Of those that a mesh axis runs over, the one named last changes fastest.
Arguments:
- tokens: bfloat16 [32768, 960], P(('fsdp', 'dp')), may hold values from -6 to 6
- seq_lengths: int32 [32, 8], P(('fsdp', 'dp')), may hold values from 0 to 1024, as said below
- norm1_gain: bfloat16 [960], P('fsdp'), may hold values from 0.5 to 1.5
- q_weight: bfloat16 [960, 960], P('fsdp', 'dp'), may hold values from -0.1875 to 0.1875
- k_weight: bfloat16 [960, 320], P('fsdp', 'dp'), may hold values from -0.1875 to 0.1875
- v_weight: bfloat16 [960, 320], P('fsdp', 'dp'), may hold values from -0.1875 to 0.1875
- o_weight: bfloat16 [960, 960], P('fsdp', 'dp'), may hold values from -0.75 to 0.75
- norm2_gain: bfloat16 [960], P('fsdp'), may hold values from 0.5 to 1.5
- gate_weight: bfloat16 [960, 2560], P('fsdp', 'dp'), may hold values from -0.1875 to 0.1875
- up_weight: bfloat16 [960, 2560], P('fsdp', 'dp'), may hold values from -0.1875 to 0.1875
- down_weight: bfloat16 [2560, 960], P('fsdp', 'dp'), may hold values from -0.125 to 0.125
- cotangent: bfloat16 [32768, 960], P(('fsdp', 'dp')), may hold values from -6 to 6
Outputs:
- mixed: bfloat16 [32768, 960], P(('fsdp', 'dp'))
- grad_tokens: float32 [32768, 960], P(('fsdp', 'dp'))
- grad_norm1: float32 [960], P('fsdp')
- grad_q: float32 [960, 960], P('fsdp', 'dp')
- grad_k: float32 [960, 320], P('fsdp', 'dp')
- grad_v: float32 [960, 320], P('fsdp', 'dp')
- grad_o: float32 [960, 960], P('fsdp', 'dp')
- grad_norm2: float32 [960], P('fsdp')
- grad_gate: float32 [960, 2560], P('fsdp', 'dp')
- grad_up: float32 [960, 2560], P('fsdp', 'dp')
- grad_down: float32 [2560, 960], P('fsdp', 'dp')
Inputs may be any that keep to these rules, and one draw needn't show every extreme that they name: `seq_lengths`: row d lists the lengths of the sequences packed one after another from the first of device d's 1024 slots; a length may be 0; a row sums to at most 1024, the rest of the slots being padding; in every draw some device holds a single sequence of exactly 1024 tokens.
All inputs are finite; a program needn't handle non-finite values.
Results may differ from a plain program's by a relative error of at most 0.017.
Values may be sent and summed in bfloat16 or wider, within the bound.
No kernel may reach another device: no remote copies, remote signals or barrier semaphores. Data moves between devices by JAX's collectives and lax.ppermute only.
A program may use at most 256 MiB of HBM per device.

v0:
```python
import math

import jax
import jax.numpy as jnp
from jax import lax
from jax.sharding import PartitionSpec as P

QUERY_HEADS = 15
KEY_VALUE_HEADS = 5
HEAD_SIZE = 64
QUERY_BLOCK_ROWS = 512


epsilon = 1e-05
rope_base = 100000.0
masked_fill = -1e30


def layout(lengths_row, n_slots):
    ends = jnp.cumsum(lengths_row)
    places = jnp.arange(n_slots, dtype=jnp.int32)
    passed = (places[:, None] >= ends[None, :]).astype(jnp.int32)
    segment = jnp.sum(passed, axis=1)
    starts = jnp.sum(passed * lengths_row[None, :], axis=1)
    live_total = ends[-1]
    return (segment, places - starts, (places < live_total).astype(jnp.float32), live_total)


def rope_tables(position):
    halfway = HEAD_SIZE // 2
    exponent = jnp.arange(halfway, dtype=jnp.float32) * (2.0 / HEAD_SIZE)
    inverse = jnp.exp(-math.log(rope_base) * exponent)
    angle = position.astype(jnp.float32)[:, None] * inverse[None, :]
    return (jnp.cos(angle), jnp.sin(angle))


def apply_rotary(values, cosine_table, sine_table):
    halfway = HEAD_SIZE // 2
    first_half = values[..., :halfway]
    second_half = values[..., halfway:]
    cos_wide = cosine_table[:, None, :]
    sin_wide = sine_table[:, None, :]
    return jnp.concatenate(
        [
            first_half * cos_wide - second_half * sin_wide,
            second_half * cos_wide + first_half * sin_wide,
        ],
        axis=-1,
    )


def inverse_rotary(grads, cosine_table, sine_table):
    halfway = HEAD_SIZE // 2
    first_half = grads[..., :halfway]
    second_half = grads[..., halfway:]
    cos_wide = cosine_table[:, None, :]
    sin_wide = sine_table[:, None, :]
    return jnp.concatenate(
        [
            first_half * cos_wide + second_half * sin_wide,
            second_half * cos_wide - first_half * sin_wide,
        ],
        axis=-1,
    )


def norm_scale(values):
    return lax.rsqrt(jnp.mean(values * values, axis=1, keepdims=True) + epsilon)


def norm_back(values, scale_rows, gain_wide, upstream):
    weighted = gain_wide[None, :] * upstream
    return scale_rows * weighted - values * scale_rows**3 * jnp.mean(
        weighted * values, axis=1, keepdims=True
    )


def block_scores(query_block_rows, key_rows, seg_query, seg_keys, starting_row, score_scale):
    scores = (
        jnp.einsum("tngd,und->ngtu", query_block_rows, key_rows, preferred_element_type=jnp.float32)
        * score_scale
    )
    query_place = starting_row + jnp.arange(query_block_rows.shape[0])
    key_place = jnp.arange(key_rows.shape[0])
    allowed = (seg_query[:, None] == seg_keys[None, :]) & (
        key_place[None, :] <= query_place[:, None]
    )
    return jnp.where(allowed[None, None], scores, masked_fill)


def shards(
    tokens,
    seq_lengths,
    norm1_gain,
    q_weight,
    k_weight,
    v_weight,
    o_weight,
    norm2_gain,
    gate_weight,
    up_weight,
    down_weight,
    cotangent,
):
    row_count = tokens.shape[0]
    dp_count = lax.axis_size("dp")
    heads_per_group = QUERY_HEADS // KEY_VALUE_HEADS
    score_scale = 1.0 / math.sqrt(HEAD_SIZE)
    n_blocks = row_count // QUERY_BLOCK_ROWS
    segment, position, live_rows, live_total = layout(seq_lengths[0], row_count)
    cosine_table, sine_table = rope_tables(position)
    attn_local = (
        lax.all_gather(q_weight, "dp", axis=1, tiled=True),
        lax.all_gather(k_weight, "dp", axis=1, tiled=True),
        lax.all_gather(v_weight, "dp", axis=1, tiled=True),
        lax.all_gather(o_weight, "dp", axis=1, tiled=True),
    )
    gain_one, query_full, key_full, value_full, output_full = (
        lax.all_gather(norm1_gain, "fsdp", axis=0, tiled=True),
        lax.all_gather(attn_local[0], "fsdp", axis=0, tiled=True),
        lax.all_gather(attn_local[1], "fsdp", axis=0, tiled=True),
        lax.all_gather(attn_local[2], "fsdp", axis=0, tiled=True),
        lax.all_gather(attn_local[3], "fsdp", axis=0, tiled=True),
    )
    q_width = query_full.shape[1]
    tokens_wide = tokens.astype(jnp.float32)
    scale_one = norm_scale(tokens_wide)
    normed_one = (tokens_wide * scale_one * gain_one.astype(jnp.float32)[None, :]).astype(
        jnp.bfloat16
    )
    query_proj = jnp.dot(normed_one, query_full, preferred_element_type=jnp.float32)
    key_projection = jnp.dot(normed_one, key_full, preferred_element_type=jnp.float32)
    value_projection = jnp.dot(normed_one, value_full, preferred_element_type=jnp.float32)
    rotated_query = apply_rotary(
        query_proj.reshape(row_count, QUERY_HEADS, HEAD_SIZE), cosine_table, sine_table
    ).astype(jnp.bfloat16)
    rotated_key = apply_rotary(
        key_projection.reshape(row_count, KEY_VALUE_HEADS, HEAD_SIZE), cosine_table, sine_table
    ).astype(jnp.bfloat16)
    value_row_slice = value_projection.astype(jnp.bfloat16).reshape(
        row_count, KEY_VALUE_HEADS, HEAD_SIZE
    )
    attended_parts = []
    lse_parts = []
    for block_index in range(n_blocks):
        starting_row = block_index * QUERY_BLOCK_ROWS
        ending_row = starting_row + QUERY_BLOCK_ROWS

        def forward_block(starting_row=starting_row, ending_row=ending_row):
            query_block_rows = rotated_query[starting_row:ending_row].reshape(
                QUERY_BLOCK_ROWS, KEY_VALUE_HEADS, heads_per_group, HEAD_SIZE
            )
            scores = block_scores(
                query_block_rows,
                rotated_key[:ending_row],
                segment[starting_row:ending_row],
                segment[:ending_row],
                starting_row,
                score_scale,
            )
            peak_score = jnp.max(scores, axis=-1, keepdims=True)
            exp_scores = jnp.exp(scores - peak_score)
            total_exp = jnp.sum(exp_scores, axis=-1, keepdims=True)
            probs_low = (exp_scores / total_exp).astype(jnp.bfloat16)
            heads_out = jnp.einsum(
                "ngtu,und->tngd",
                probs_low,
                value_row_slice[:ending_row],
                preferred_element_type=jnp.float32,
            )
            return (
                heads_out.reshape(QUERY_BLOCK_ROWS, q_width),
                (peak_score + jnp.log(total_exp))[..., 0],
            )

        heads_out, lse_block = forward_block()
        attended_parts.append(heads_out)
        lse_parts.append(lse_block)
    attended = jnp.concatenate(attended_parts, axis=0).astype(jnp.bfloat16)
    row_lse = jnp.concatenate(lse_parts, axis=2)
    branch_one = jnp.dot(attended, output_full, preferred_element_type=jnp.float32)
    hidden_mid = tokens_wide + branch_one
    ffn_local = (
        lax.all_gather(gate_weight, "dp", axis=1, tiled=True),
        lax.all_gather(up_weight, "dp", axis=1, tiled=True),
        lax.all_gather(down_weight, "dp", axis=1, tiled=True),
    )
    gain_two, gate_full, up_full, down_full = (
        lax.all_gather(norm2_gain, "fsdp", axis=0, tiled=True),
        lax.all_gather(ffn_local[0], "fsdp", axis=0, tiled=True),
        lax.all_gather(ffn_local[1], "fsdp", axis=0, tiled=True),
        lax.all_gather(ffn_local[2], "fsdp", axis=0, tiled=True),
    )
    scale_two = norm_scale(hidden_mid)
    normed_two = (hidden_mid * scale_two * gain_two.astype(jnp.float32)[None, :]).astype(
        jnp.bfloat16
    )
    gate_proj = jnp.dot(normed_two, gate_full, preferred_element_type=jnp.float32)
    up_proj = jnp.dot(normed_two, up_full, preferred_element_type=jnp.float32)
    sigma_gate = jax.nn.sigmoid(gate_proj)
    silu_gate = gate_proj * sigma_gate
    hidden_ff = (silu_gate * up_proj).astype(jnp.bfloat16)
    branch_two = jnp.dot(hidden_ff, down_full, preferred_element_type=jnp.float32)
    mixed = (live_rows[:, None] * (hidden_mid + branch_two)).astype(jnp.bfloat16)
    again_local = (
        lax.all_gather(q_weight, "dp", axis=1, tiled=True),
        lax.all_gather(k_weight, "dp", axis=1, tiled=True),
        lax.all_gather(v_weight, "dp", axis=1, tiled=True),
        lax.all_gather(o_weight, "dp", axis=1, tiled=True),
        lax.all_gather(gate_weight, "dp", axis=1, tiled=True),
        lax.all_gather(up_weight, "dp", axis=1, tiled=True),
        lax.all_gather(down_weight, "dp", axis=1, tiled=True),
    )
    (
        gain_one,
        query_full,
        key_full,
        value_full,
        output_full,
        gain_two,
        gate_full,
        up_full,
        down_full,
    ) = (
        lax.all_gather(norm1_gain, "fsdp", axis=0, tiled=True),
        lax.all_gather(again_local[0], "fsdp", axis=0, tiled=True),
        lax.all_gather(again_local[1], "fsdp", axis=0, tiled=True),
        lax.all_gather(again_local[2], "fsdp", axis=0, tiled=True),
        lax.all_gather(again_local[3], "fsdp", axis=0, tiled=True),
        lax.all_gather(norm2_gain, "fsdp", axis=0, tiled=True),
        lax.all_gather(again_local[4], "fsdp", axis=0, tiled=True),
        lax.all_gather(again_local[5], "fsdp", axis=0, tiled=True),
        lax.all_gather(again_local[6], "fsdp", axis=0, tiled=True),
    )
    gain_one_wide = gain_one.astype(jnp.float32)
    gain_two_wide = gain_two.astype(jnp.float32)
    grad_mixed = live_rows[:, None] * cotangent.astype(jnp.float32)
    grad_low = grad_mixed.astype(jnp.bfloat16)
    grad_down = jnp.einsum("tf,td->fd", hidden_ff, grad_low, preferred_element_type=jnp.float32)
    grad_hidden = jnp.einsum("td,fd->tf", grad_low, down_full, preferred_element_type=jnp.float32)
    grad_gate_low = (
        grad_hidden * up_proj * sigma_gate * (1.0 + gate_proj * (1.0 - sigma_gate))
    ).astype(jnp.bfloat16)
    grad_up_low = (grad_hidden * silu_gate).astype(jnp.bfloat16)
    grad_gate = jnp.einsum(
        "td,tf->df", normed_two, grad_gate_low, preferred_element_type=jnp.float32
    )
    grad_up = jnp.einsum("td,tf->df", normed_two, grad_up_low, preferred_element_type=jnp.float32)
    grad_normed_two = jnp.einsum(
        "tf,df->td", grad_gate_low, gate_full, preferred_element_type=jnp.float32
    )
    grad_normed_two = grad_normed_two + jnp.einsum(
        "tf,df->td", grad_up_low, up_full, preferred_element_type=jnp.float32
    )
    grad_gain_two = jnp.sum(grad_normed_two * hidden_mid * scale_two, axis=0)
    grad_mid = grad_mixed + norm_back(hidden_mid, scale_two, gain_two_wide, grad_normed_two)
    grad_branch = grad_mid.astype(jnp.bfloat16)
    grad_output = jnp.einsum("tq,td->qd", attended, grad_branch, preferred_element_type=jnp.float32)
    attention_gradient = jnp.einsum(
        "td,qd->tq", grad_branch, output_full, preferred_element_type=jnp.float32
    ).astype(jnp.bfloat16)
    query_grads = []
    key_accumulator = jnp.zeros((row_count, KEY_VALUE_HEADS, HEAD_SIZE), jnp.float32)
    value_accumulator = jnp.zeros((row_count, KEY_VALUE_HEADS, HEAD_SIZE), jnp.float32)
    for block_index in range(n_blocks):
        starting_row = block_index * QUERY_BLOCK_ROWS
        ending_row = starting_row + QUERY_BLOCK_ROWS

        def backward_block(starting_row=starting_row, ending_row=ending_row):
            query_block_rows = rotated_query[starting_row:ending_row].reshape(
                QUERY_BLOCK_ROWS, KEY_VALUE_HEADS, heads_per_group, HEAD_SIZE
            )
            block_gradient = attention_gradient[starting_row:ending_row].reshape(
                QUERY_BLOCK_ROWS, KEY_VALUE_HEADS, heads_per_group, HEAD_SIZE
            )
            scores = block_scores(
                query_block_rows,
                rotated_key[:ending_row],
                segment[starting_row:ending_row],
                segment[:ending_row],
                starting_row,
                score_scale,
            )
            attn_probs = jnp.exp(scores - row_lse[:, :, starting_row:ending_row, None])
            probs_low = attn_probs.astype(jnp.bfloat16)
            grad_probs = jnp.einsum(
                "tngd,und->ngtu",
                block_gradient,
                value_row_slice[:ending_row],
                preferred_element_type=jnp.float32,
            )
            row_dot = jnp.sum(attn_probs * grad_probs, axis=-1, keepdims=True)
            grad_scores = (attn_probs * (grad_probs - row_dot)).astype(jnp.bfloat16)
            grad_query = (
                jnp.einsum(
                    "ngtu,und->tngd",
                    grad_scores,
                    rotated_key[:ending_row],
                    preferred_element_type=jnp.float32,
                )
                * score_scale
            )
            grad_key = (
                jnp.einsum(
                    "ngtu,tngd->und",
                    grad_scores,
                    query_block_rows,
                    preferred_element_type=jnp.float32,
                )
                * score_scale
            )
            grad_value = jnp.einsum(
                "ngtu,tngd->und", probs_low, block_gradient, preferred_element_type=jnp.float32
            )
            return (
                grad_query.reshape(QUERY_BLOCK_ROWS, QUERY_HEADS, HEAD_SIZE),
                grad_key,
                grad_value,
            )

        grad_query, grad_key, grad_value = backward_block()
        query_grads.append(grad_query)
        key_accumulator = key_accumulator.at[:ending_row].add(grad_key)
        value_accumulator = value_accumulator.at[:ending_row].add(grad_value)
    grad_query_rot = jnp.concatenate(query_grads, axis=0)
    grad_query_low = (
        inverse_rotary(grad_query_rot, cosine_table, sine_table)
        .astype(jnp.bfloat16)
        .reshape(row_count, q_width)
    )
    key_gradient_reduced = (
        inverse_rotary(key_accumulator, cosine_table, sine_table)
        .astype(jnp.bfloat16)
        .reshape(row_count, KEY_VALUE_HEADS * HEAD_SIZE)
    )
    value_gradient_reduced = value_accumulator.astype(jnp.bfloat16).reshape(
        row_count, KEY_VALUE_HEADS * HEAD_SIZE
    )
    grad_qw = jnp.einsum(
        "td,tq->dq", normed_one, grad_query_low, preferred_element_type=jnp.float32
    )
    grad_kw = jnp.einsum(
        "td,tq->dq", normed_one, key_gradient_reduced, preferred_element_type=jnp.float32
    )
    grad_vw = jnp.einsum(
        "td,tq->dq", normed_one, value_gradient_reduced, preferred_element_type=jnp.float32
    )
    grad_normed_one = jnp.einsum(
        "tq,dq->td", grad_query_low, query_full, preferred_element_type=jnp.float32
    )
    grad_normed_one = grad_normed_one + jnp.einsum(
        "tq,dq->td", key_gradient_reduced, key_full, preferred_element_type=jnp.float32
    )
    grad_normed_one = grad_normed_one + jnp.einsum(
        "tq,dq->td", value_gradient_reduced, value_full, preferred_element_type=jnp.float32
    )
    grad_gain_one = jnp.sum(grad_normed_one * tokens_wide * scale_one, axis=0)
    grad_tokens = grad_mid + norm_back(tokens_wide, scale_one, gain_one_wide, grad_normed_one)
    row_sums = (
        lax.psum_scatter(grad_gain_one, "fsdp", scatter_dimension=0, tiled=True),
        lax.psum_scatter(grad_qw, "fsdp", scatter_dimension=0, tiled=True),
        lax.psum_scatter(grad_kw, "fsdp", scatter_dimension=0, tiled=True),
        lax.psum_scatter(grad_vw, "fsdp", scatter_dimension=0, tiled=True),
        lax.psum_scatter(grad_output, "fsdp", scatter_dimension=0, tiled=True),
        lax.psum_scatter(grad_gain_two, "fsdp", scatter_dimension=0, tiled=True),
        lax.psum_scatter(grad_gate, "fsdp", scatter_dimension=0, tiled=True),
        lax.psum_scatter(grad_up, "fsdp", scatter_dimension=0, tiled=True),
        lax.psum_scatter(grad_down, "fsdp", scatter_dimension=0, tiled=True),
    )
    tiled_one = jnp.broadcast_to(row_sums[0][:, None], (row_sums[0].shape[0], dp_count))
    tiled_two = jnp.broadcast_to(row_sums[5][:, None], (row_sums[5].shape[0], dp_count))
    final_sums = (
        lax.psum_scatter(
            tiled_one.astype(jnp.bfloat16), "dp", scatter_dimension=1, tiled=True
        ).astype(jnp.float32),
        lax.psum_scatter(
            row_sums[1].astype(jnp.bfloat16), "dp", scatter_dimension=1, tiled=True
        ).astype(jnp.float32),
        lax.psum_scatter(
            row_sums[2].astype(jnp.bfloat16), "dp", scatter_dimension=1, tiled=True
        ).astype(jnp.float32),
        lax.psum_scatter(
            row_sums[3].astype(jnp.bfloat16), "dp", scatter_dimension=1, tiled=True
        ).astype(jnp.float32),
        lax.psum_scatter(
            row_sums[4].astype(jnp.bfloat16), "dp", scatter_dimension=1, tiled=True
        ).astype(jnp.float32),
        lax.psum_scatter(
            tiled_two.astype(jnp.bfloat16), "dp", scatter_dimension=1, tiled=True
        ).astype(jnp.float32),
        lax.psum_scatter(
            row_sums[6].astype(jnp.bfloat16), "dp", scatter_dimension=1, tiled=True
        ).astype(jnp.float32),
        lax.psum_scatter(
            row_sums[7].astype(jnp.bfloat16), "dp", scatter_dimension=1, tiled=True
        ).astype(jnp.float32),
        lax.psum_scatter(
            row_sums[8].astype(jnp.bfloat16), "dp", scatter_dimension=1, tiled=True
        ).astype(jnp.float32),
    )
    gain_sum_one = final_sums[0].reshape(-1)
    gain_sum_two = final_sums[5].reshape(-1)
    return (
        mixed,
        grad_tokens,
        gain_sum_one,
        final_sums[1],
        final_sums[2],
        final_sums[3],
        final_sums[4],
        gain_sum_two,
        final_sums[6],
        final_sums[7],
        final_sums[8],
    )


def solution(mesh):
    return jax.shard_map(
        shards,
        mesh=mesh,
        in_specs=(
            P(("fsdp", "dp"), None),
            P(("fsdp", "dp"), None),
            P("fsdp"),
            P("fsdp", "dp"),
            P("fsdp", "dp"),
            P("fsdp", "dp"),
            P("fsdp", "dp"),
            P("fsdp"),
            P("fsdp", "dp"),
            P("fsdp", "dp"),
            P("fsdp", "dp"),
            P(("fsdp", "dp"), None),
        ),
        out_specs=(
            P(("fsdp", "dp"), None),
            P(("fsdp", "dp"), None),
            P("fsdp"),
            P("fsdp", "dp"),
            P("fsdp", "dp"),
            P("fsdp", "dp"),
            P("fsdp", "dp"),
            P("fsdp"),
            P("fsdp", "dp"),
            P("fsdp", "dp"),
            P("fsdp", "dp"),
        ),
        check_vma=False,
    )
```

profile of v0, /device:TPU:0, one launch (start us, length us, event | category | flops | bytes accessed | tf_op | source)
XLA Modules:
  0.0 1358.9 jit_solution(1392987357691843995)
XLA Ops:
  8.2 7.1 all_gather.69
  17.2 5.9 all_gather.71
  24.0 9.9 all_gather.76
  34.0 8.8 all_gather.74
  42.9 8.0 all-gather.2
  55.4 21.8 %all-reduce.11 = (bf16[960]{0:T(1024)(128)(2,1)S(1)}, bf16[960]{0:T(1024)(128)(2,1)S(1)}) all-reduce(bf16[960]{0:T(1024)(128)(2,1)S(1)} %dynamic-update-slice.10, bf16[960]{0:T(1024)(128)(2,1)S(1)} %dynamic-update-slice.11), channel_id=1, replica_groups=mesh['fsdp'=8,'dp'=4] {'fsdp'}, use_global_device_ids=true, to_apply=%add.2 | all-reduce | flops 1920 | bytes 7680
  79.0 5.3 all_gather.67
  84.3 5.3 all_gather.65
  90.5 33.3 %all-gather = bf16[8,120,320]{1,2,0:T(8,128)(2,1)S(1)} all-gather(bf16[1,120,320]{1,2,0:T(8,128)(2,1)S(1)} %bitcast.225), channel_id=1, replica_groups=mesh['fsdp'=8,'dp'=4] {'fsdp'}, dimensions={0}, use_global_device_ids=true | all-gather | bytes 691200 | tf_op jit(solution)/shard_map/all_gather | solution.py:122
  124.8 33.5 %all-gather.1 = bf16[8,120,320]{1,2,0:T(8,128)(2,1)S(1)} all-gather(bf16[1,120,320]{1,2,0:T(8,128)(2,1)S(1)} %bitcast.224), channel_id=1, replica_groups=mesh['fsdp'=8,'dp'=4] {'fsdp'}, dimensions={0}, use_global_device_ids=true | all-gather | bytes 691200 | tf_op jit(solution)/shard_map/all_gather | solution.py:121
  170.7 7.0 fusion.92
  177.7 7.8 fusion.12
  185.5 8.1 fusion.35
  193.6 12.9 fusion.91
  206.5 12.9 fusion.3
  219.4 14.1 %fusion.36 = bf16[5,64,3,512]{3,1,2,0:T(8,128)(2,1)} fusion(bf16[1024,5,64,1]{0,2,3,1:T(8,128)(2,1)S(1)} %bitcast.219, f32[5,3,512,1024]{2,3,1,0:T(8,128)} %get-tuple-element.115, f32[5,3,512]{2,1,0:T(4,128)S(1)} %fusion.3, f32[5,3,512]{2,1,0:T(4,128)S(1)} %get-tuple-element.114), kind=kOutput, calls=%fused_computation.78 | convolution fusion | flops 1030717440 | bytes 33157120 | tf_op jit(solution)/shard_map/ngtu,und->tngd/dot_general | solution.py:165
  241.5 10.6 fusion.94
  252.0 41.3 %all-gather.13.cloned.1.call-done = bf16[960,2560]{1,0:T(8,128)(2,1)} async-done(((bf16[120,2560]{1,0:T(8,128)(2,1)}), bf16[960,2560]{1,0:T(8,128)(2,1)}) %all-gather.13.cloned.1.call-update) | async-done | bytes 4915216 | tf_op jit(solution)/shard_map/all_gather | solution.py:190
  293.3 10.9 fusion.93
  304.3 75.6 %all-gather.17.cloned.1.call-done = bf16[2560,960]{1,0:T(8,128)(2,1)} async-done(((bf16[320,960]{1,0:T(8,128)(2,1)}), bf16[2560,960]{1,0:T(8,128)(2,1)}) %all-gather.17.cloned.1.call-update) | async-done | bytes 4915216 | tf_op jit(solution)/shard_map/all_gather | solution.py:192
  379.9 18.6 %multiply_convert_fusion = (bf16[1024,2560]{1,0:T(8,128)(2,1)}, bf16[1024,2560]{1,0:T(8,128)(2,1)}, bf16[1024,2560]{1,0:T(8,128)(2,1)}) fusion(f32[1024,2560]{1,0:T(8,128)} %fusion.93, f32[1024,2560]{1,0:T(8,128)} %fusion.94, bf16[2560,960]{1,0:T(8,128)(2,1)} %all-gather.17.cloned.1.call-done, bf16[1024,960]{0,1:T(8,128)(2,1)S(1)} %copy-done.29, ...), kind=kOutput, calls=%fused_computation.25 | convolution fusion | flops 5075435520 | bytes 43585536 | tf_op jit(solution)/shard_map/td,fd->tf/dot_general | solution.py:240
  398.5 9.0 fusion.95
  407.5 8.9 multiply_reduce_fusion
  429.1 13.5 fusion.7
  444.6 7.7 fusion.9
  455.5 23.8 %fusion = (f32[5,3,512]{2,1,0:T(4,128)S(1)}, f32[5,1024,512,3]{2,1,3,0:T(8,128)}) fusion(f32[5,3,512,1024]{2,3,1,0:T(8,128)} %get-tuple-element.115, f32[5,3,512]{2,1,0:T(4,128)S(1)} %log_add_fusion, bf16[1024,5,64,1]{0,2,3,1:T(8,128)(2,1)S(1)} %bitcast.220, bf16[512,5,3,64]{0,3,2,1:T(8,128)(2,1)S(1)} %bitcast.202), kind=kOutput, calls=%fused_computation.2 | convolution fusion | flops 1030218240 | bytes 64614400 | tf_op jit(solution)/shard_map/tngd,und->ngtu/dot_general | solution.py:286
  479.3 27.1 %fusion.2 = bf16[5,3,512,1024]{2,3,1,0:T(8,128)(2,1)} fusion(f32[5,1024,512,3]{2,1,3,0:T(8,128)} %get-tuple-element.122, f32[5,3,512,1024]{2,3,1,0:T(8,128)} %get-tuple-element.115, f32[5,3,512]{2,1,0:T(4,128)S(1)} %get-tuple-element.121, f32[5,3,512]{2,1,0:T(4,128)S(1)} %log_add_fusion), kind=kLoop, calls=%fused_computation.4 | loop fusion | flops 31457280 | bytes 78704640 | tf_op jit(solution)/shard_map/convert_element_type | solution.py:293
  506.5 8.4 convolution_multiply_fusion
  521.3 10.8 fusion.98
  532.2 10.5 fusion.97
  542.7 10.6 fusion.31
  554.1 9.1 fusion.49
  563.2 13.2 fusion.43
  578.5 6.6 fusion.53
  585.1 10.4 fusion.48
  606.1 146.5 %all-reduce.14 = (bf16[960]{0:T(1024)(128)(2,1)S(1)}, bf16[960,320]{0,1:T(8,128)(2,1)}, bf16[960,320]{0,1:T(8,128)(2,1)}, bf16[960]{0:T(1024)(128)(2,1)S(1)}) all-reduce(f32[960]{0:T(1024)S(1)} %get-tuple-element.77, f32[960,320]{0,1:T(8,128)} %fusion.79, ...), channel_id=2, replica_groups=mesh['fsdp'=8,'dp'=4] {'fsdp'}, use_global_device_ids=true, to_apply=%region_14.15.clone | all-reduce | flops 616320 | bytes 3697920
  760.0 72.9 %reduce-scatter.35.cloned.1.call-done = f32[120,2560]{1,0:T(8,128)} async-done(((f32[960,2560]{1,0:T(8,128)}), f32[120,2560]{1,0:T(8,128)}) %reduce-scatter.35.cloned.1.call-update) | async-done | bytes 1228816 | tf_op jit(solution)/shard_map/reduce_scatter | solution.py:367
  835.5 169.1 %reduce-scatter.33.cloned.1.call-done = f32[120,2560]{1,0:T(8,128)} async-done(((f32[960,2560]{1,0:T(8,128)}), f32[120,2560]{1,0:T(8,128)}) %reduce-scatter.33.cloned.1.call-update) | async-done | bytes 1228816 | tf_op jit(solution)/shard_map/reduce_scatter | solution.py:366
  1007.7 177.5 %reduce-scatter.37.cloned.1.call-done = f32[320,960]{1,0:T(8,128)} async-done(((f32[2560,960]{1,0:T(8,128)}), f32[320,960]{1,0:T(8,128)}) %reduce-scatter.37.cloned.1.call-update) | async-done | bytes 1228816 | tf_op jit(solution)/shard_map/reduce_scatter | solution.py:368
  1187.8 10.4 multiply_convert_fusion.3
  1198.3 6.8 all-reduce.12
  1207.5 6.2 fusion.24
  1215.0 14.2 %reduce-scatter.29.cloned.1.call-done = bf16[120,80]{0,1:T(8,128)(2,1)} async-done(((bf16[120,320]{0,1:T(8,128)(2,1)}), bf16[120,80]{0,1:T(8,128)(2,1)}) %reduce-scatter.29.cloned.1.call-update) | async-done | bytes 19216 | tf_op jit(solution)/shard_map/reduce_scatter | solution.py:382
  1230.6 21.7 %reduce-scatter.41.cloned.1.call-done = bf16[240,120]{1,0:T(8,128)(2,1)} async-done(((bf16[960,120]{1,0:T(8,128)(2,1)}), bf16[240,120]{1,0:T(8,128)(2,1)}) %reduce-scatter.41.cloned.1.call-update) | async-done | bytes 57616
  1253.8 21.5 %reduce-scatter.39.cloned.1.call-done = bf16[240,120]{1,0:T(8,128)(2,1)} async-done(((bf16[960,120]{1,0:T(8,128)(2,1)}), bf16[240,120]{1,0:T(8,128)(2,1)}) %reduce-scatter.39.cloned.1.call-update) | async-done | bytes 57616
  1276.9 23.2 %reduce-scatter.45.cloned.1.call-done = bf16[640,120]{1,0:T(8,128)(2,1)} async-done(((bf16[2560,120]{1,0:T(8,128)(2,1)}), bf16[640,120]{1,0:T(8,128)(2,1)}) %reduce-scatter.45.cloned.1.call-update) | async-done | bytes 153616
  1301.9 23.0 %reduce-scatter.43.cloned.1.call-done = bf16[640,120]{1,0:T(8,128)(2,1)} async-done(((bf16[2560,120]{1,0:T(8,128)(2,1)}), bf16[640,120]{1,0:T(8,128)(2,1)}) %reduce-scatter.43.cloned.1.call-update) | async-done | bytes 153616
  1326.8 23.5 %reduce-scatter.47.cloned.1.call-done = bf16[240,320]{1,0:T(8,128)(2,1)} async-done(((bf16[960,320]{1,0:T(8,128)(2,1)}), bf16[240,320]{1,0:T(8,128)(2,1)}) %reduce-scatter.47.cloned.1.call-update) | async-done | bytes 153616
  (250 shorter events, 97.6 us)
Async XLA Ops:
  7.2 35.7 %copy-start.37 = (bf16[320,240]{1,0:T(8,128)(2,1)S(1)}, bf16[320,240]{1,0:T(8,128)(2,1)}, u32[]{:S(2)}) copy-start(bf16[320,240]{1,0:T(8,128)(2,1)} %param.34) | copy-start | bytes 460804
  7.2 158.2 %all-gather.9.cloned.1.call-start = ((), (), s32[]{:S(2)}) async-start(), calls=%async_computation.12 | async-start | bytes 2211840 | tf_op jit(solution)/shard_map/all_gather | solution.py:120
  16.2 217.4 %all-gather.11.cloned.1.call-start = ((), (), s32[]{:S(2)}) async-start(), calls=%async_computation.13 | async-start | bytes 2211840 | tf_op jit(solution)/shard_map/all_gather | solution.py:123
  17.2 35.7 %copy-start.47 = (s32[1,8]{1,0:T(1,128)S(1)}, s32[1,8]{1,0:T(1,128)}, u32[]{:S(2)}) copy-start(s32[1,8]{1,0:T(1,128)} %param.25) | copy-start | bytes 100
  17.2 36.5 %copy-start.46 = (u32[32]{0:T(128)S(1)}, u32[32]{0:T(128)}, u32[]{:S(2)}) copy-start(u32[32]{0:T(128)} %constant.152) | copy-start | bytes 388
  17.2 37.7 %copy-start.50 = (bf16[120]{0:T(256)(128)(2,1)S(1)}, bf16[120]{0:T(256)(128)(2,1)}, u32[]{:S(2)}) copy-start(bf16[120]{0:T(256)(128)(2,1)} %param.26) | copy-start | bytes 724
  17.2 37.9 %copy-start.51 = (bf16[120]{0:T(256)(128)(2,1)S(1)}, bf16[120]{0:T(256)(128)(2,1)}, u32[]{:S(2)}) copy-start(bf16[120]{0:T(256)(128)(2,1)} %param.31) | copy-start | bytes 724
  17.2 60.6 %copy-start.1 = (bf16[1024,960]{0,1:T(8,128)(2,1)S(1)}, bf16[1024,960]{0,1:T(8,128)(2,1)}, u32[]{:S(2)}) copy-start(bf16[1024,960]{0,1:T(8,128)(2,1)} %param.24) | copy-start | bytes 5898244
  24.0 216.2 %all-gather.15.cloned.1.call-start = ((), (), s32[]{:S(2)}) async-start(), calls=%async_computation.15 | async-start | bytes 5529600 | tf_op jit(solution)/shard_map/all_gather | solution.py:191
  34.0 45.1 %copy-start.42 = (bf16[120,80]{0,1:T(8,128)(2,1)S(1)}, bf16[120,80]{0,1:T(8,128)(2,1)}, u32[]{:S(2)}) copy-start(bf16[120,80]{0,1:T(8,128)(2,1)} %param.28) | copy-start | bytes 57604
  34.0 50.4 %copy-start.43 = (bf16[120,80]{0,1:T(8,128)(2,1)S(1)}, bf16[120,80]{0,1:T(8,128)(2,1)}, u32[]{:S(2)}) copy-start(bf16[120,80]{0,1:T(8,128)(2,1)} %param.29) | copy-start | bytes 57604
  34.0 259.4 %all-gather.13.cloned.1.call-start = ((), (), s32[]{:S(2)}) async-start(), calls=%async_computation.14 | async-start | bytes 5529600 | tf_op jit(solution)/shard_map/all_gather | solution.py:190
  42.8 337.0 %all-gather.17.cloned.1.call-start = ((), (), s32[]{:S(2)}) async-start(), calls=%async_computation.16 | async-start | bytes 5898240 | tf_op jit(solution)/shard_map/all_gather | solution.py:192
  52.8 703.2 %reduce-scatter.31.cloned.1.call-start = ((), (), s32[]{:S(2)}) async-start(), calls=%async_computation.20 | async-start | bytes 4423680 | tf_op jit(solution)/shard_map/reduce_scatter | solution.py:364
  77.2 88.2 %copy-start.40 = (f32[960]{0:T(1024)}, f32[960]{0:T(1024)S(1)}, u32[]{:S(2)}) copy-start(f32[960]{0:T(1024)S(1)} %convert_element_type.149) | copy-start | bytes 11524
  78.9 86.5 %copy-start.38 = (f32[1024]{0:T(1024)}, f32[1024]{0:T(1024)S(1)}, u32[]{:S(2)}) copy-start(f32[1024]{0:T(1024)S(1)} %get-tuple-element.107) | copy-start | bytes 12292
  124.8 37.5 %copy-start.22 = (bf16[960,320]{0,1:T(8,128)(2,1)}, bf16[960,320]{0,1:T(8,128)(2,1)S(1)}, u32[]{:S(2)}) copy-start(bf16[960,320]{0,1:T(8,128)(2,1)S(1)} %reshape.459) | copy-start | bytes 1843204
  165.4 28.3 %copy-start.12 = (bf16[1024,5,32]{0,2,1:T(8,128)(2,1)}, bf16[1024,5,32]{0,2,1:T(8,128)(2,1)S(1)}, u32[]{:S(2)}) copy-start(bf16[1024,5,32]{0,2,1:T(8,128)(2,1)S(1)} %get-tuple-element.102) | copy-start | bytes 983044
  165.4 28.2 %copy-start.14 = (bf16[1024,5,32]{0,2,1:T(8,128)(2,1)}, bf16[1024,5,32]{0,2,1:T(8,128)(2,1)S(1)}, u32[]{:S(2)}) copy-start(bf16[1024,5,32]{0,2,1:T(8,128)(2,1)S(1)} %get-tuple-element.103) | copy-start | bytes 983044
  170.6 23.0 %copy-start.8 = (bf16[512,15,64]{0,2,1:T(8,128)(2,1)}, bf16[512,15,64]{0,2,1:T(8,128)(2,1)S(1)}, u32[]{:S(2)}) copy-start(bf16[512,15,64]{0,2,1:T(8,128)(2,1)S(1)} %get-tuple-element.99) | copy-start | bytes 2949124
  177.7 7.8 copy-start.27
  206.5 12.9 copy-start.34
  219.4 14.1 %copy-start.52 = (bf16[5,64,3,512]{3,1,2,0:T(8,128)(2,1)S(1)}, bf16[5,64,3,512]{3,1,2,0:T(8,128)(2,1)}, u32[]{:S(2)}) copy-start(bf16[5,64,3,512]{3,1,2,0:T(8,128)(2,1)} %fusion.35) | copy-start | bytes 2949124
  252.0 127.8 %copy-start.29 = (bf16[1024,960]{0,1:T(8,128)(2,1)S(1)}, bf16[1024,960]{0,1:T(8,128)(2,1)}, u32[]{:S(2)}) copy-start(bf16[1024,960]{0,1:T(8,128)(2,1)} %param.35) | copy-start | bytes 5898244
  398.5 9.0 copy-start.4
  398.5 9.0 copy-start.55
  428.2 27.3 %copy-start.10 = (bf16[512,960]{0,1:T(8,128)(2,1)}, bf16[512,960]{0,1:T(8,128)(2,1)S(1)}, u32[]{:S(2)}) copy-start(bf16[512,960]{0,1:T(8,128)(2,1)S(1)} %get-tuple-element.97) | copy-start | bytes 2949124
  428.3 329.8 %reduce-scatter.25.cloned.1.call-start = ((), (), s32[]{:S(2)}) async-start(), calls=%async_computation.17 | async-start | bytes 4423680 | tf_op jit(solution)/shard_map/reduce_scatter | solution.py:361
  428.3 14.3 %slice-start = ((s8[15728640]{0:T(1024)(128)(4,1)}), s8[4194304]{0:T(1024)(128)(4,1)S(1)}, s32[]{:S(2)}) async-start(s8[15728640]{0:T(1024)(128)(4,1)} %bitcast.194), calls=%async_computation.29 | async-start | bytes 8388608
  429.0 13.6 slice-start.1
  429.0 14.5 %slice-start.2 = ((s8[15728640]{0:T(1024)(128)(4,1)}), s8[4194304]{0:T(1024)(128)(4,1)S(1)}, s32[]{:S(2)}) async-start(s8[15728640]{0:T(1024)(128)(4,1)} %bitcast.194), calls=%async_computation.31 | async-start | bytes 8388608
  429.0 15.5 %slice-start.3 = ((s8[15728640]{0:T(1024)(128)(4,1)}), s8[3145728]{0:T(1024)(128)(4,1)S(1)}, s32[]{:S(2)}) async-start(s8[15728640]{0:T(1024)(128)(4,1)} %bitcast.194), calls=%async_computation.32 | async-start | bytes 6291456
  444.6 7.8 copy-start.15
  506.4 8.4 copy-start.17
  506.4 8.4 copy-start.19
  521.3 311.7 %reduce-scatter.35.cloned.1.call-start = ((), (), s32[]{:S(2)}) async-start(), calls=%async_computation.22 | async-start | bytes 11059200 | tf_op jit(solution)/shard_map/reduce_scatter | solution.py:367
  532.2 472.4 %reduce-scatter.33.cloned.1.call-start = ((), (), s32[]{:S(2)}) async-start(), calls=%async_computation.21 | async-start | bytes 11059200 | tf_op jit(solution)/shard_map/reduce_scatter | solution.py:366
  542.7 642.5 %reduce-scatter.37.cloned.1.call-start = ((), (), s32[]{:S(2)}) async-start(), calls=%async_computation.23 | async-start | bytes 11796480 | tf_op jit(solution)/shard_map/reduce_scatter | solution.py:368
  553.4 660.2 %reduce-scatter.27.cloned.1.call-start = ((), (), s32[]{:S(2)}) async-start(), calls=%async_computation.18 | async-start | bytes 102400 | tf_op jit(solution)/shard_map/reduce_scatter | solution.py:379
  554.1 9.1 copy-start.11
  754.2 475.0 %reduce-scatter.29.cloned.1.call-start = ((), (), s32[]{:S(2)}) async-start(), calls=%async_computation.19 | async-start | bytes 102400 | tf_op jit(solution)/shard_map/reduce_scatter | solution.py:382
  756.0 496.3 %reduce-scatter.41.cloned.1.call-start = ((), (), s32[]{:S(2)}) async-start(), calls=%async_computation.25 | async-start | bytes 307200
  758.0 517.3 %reduce-scatter.39.cloned.1.call-start = ((), (), s32[]{:S(2)}) async-start(), calls=%async_computation.24 | async-start | bytes 307200
  760.0 247.1 %copy-start.54 = (u32[32]{0:T(128)S(1)}, u32[32]{0:T(128)}, u32[]{:S(2)}) copy-start(u32[32]{0:T(128)} %constant.168) | copy-start | bytes 388
  760.0 540.1 %reduce-scatter.45.cloned.1.call-start = ((), (), s32[]{:S(2)}) async-start(), calls=%async_computation.27 | async-start | bytes 819200
  835.4 489.5 %reduce-scatter.43.cloned.1.call-start = ((), (), s32[]{:S(2)}) async-start(), calls=%async_computation.26 | async-start | bytes 819200
  1007.1 343.2 %reduce-scatter.47.cloned.1.call-start = ((), (), s32[]{:S(2)}) async-start(), calls=%async_computation.28 | async-start | bytes 921600
  1187.8 19.7 %copy-start.44 = (f32[1024]{0:T(1024)S(1)}, f32[1024]{0:T(1024)}, u32[]{:S(2)}) copy-start(f32[1024]{0:T(1024)} %get-tuple-element.106) | copy-start | bytes 12292
  (29 other events, 86.3 us)
Sparse Core Ops, SparseCore 0:
  16.3 49.6 all-gather.8
  68.7 54.4 all-gather.10
  125.4 85.3 all-gather.14
  212.9 80.4 all-gather.12
  295.4 84.4 all-gather.16
  428.4 82.4 reduce-scatter.30
  521.4 82.3 reduce-scatter.24
  607.4 225.5 reduce-scatter.34
  836.6 167.8 reduce-scatter.32
  1008.0 177.1 reduce-scatter.36
  1188.2 18.5 reduce-scatter.26
  1209.7 19.4 reduce-scatter.28
  1232.2 19.9 reduce-scatter.40
  1255.3 19.9 reduce-scatter.38
  1277.6 22.4 reduce-scatter.44
  1302.5 22.4 reduce-scatter.42
  1327.3 22.9 reduce-scatter.46
where the time goes:
time: 1370 us; the launch traced here: 1360 us
  waiting for transfers between devices  664 us (48%)
  blocking collectives  292 us (21%)
  matrix products  263 us (19%)
  other arithmetic  84.3 us (6%)
  local copies, waits for them, and re-layouts  38.1 us (3%)
  between operations  16.4 us (1%)
    reduce_scatter x1, waiting for transfers between devices, shards(): lax.psum_scatter(grad_down, 'fsdp', scatter_dimension=0, tiled=True)  177 us
    unnamed x3, blocking collectives  175 us
    reduce_scatter x1, waiting for transfers between devices, shards(): lax.psum_scatter(grad_gate, 'fsdp', scatter_dimension=0, tiled=True)  169 us
    unnamed x22, waiting for transfers between devices  113 us
    all_gather x1, waiting for transfers between devices, shards(): lax.all_gather(ffn_local[2], 'fsdp', axis=0, tiled=True)  75.6 us
    reduce_scatter x1, waiting for transfers between devices, shards(): lax.psum_scatter(grad_up, 'fsdp', scatter_dimension=0, tiled=True)  72.9 us
    all_gather x1, waiting for transfers between devices, shards(): lax.all_gather(ffn_local[0], 'fsdp', axis=0, tiled=True)  41.3 us
    dot_general x2, matrix products, backward_block(): jnp.einsum('tngd,und->ngtu', block_gradient, value_row_slice[:ending_row]...  37.4 us
  transfers between devices with their start and end apart: 17, of which 11 were waited for; matrix products, arithmetic and copies ran while one was open for 24% of the time, Pallas kernels for 0%

commit v1 on v0

--- a/solution.py
+++ b/solution.py
@@ -17,7 +17,8 @@
 
 
 def layout(lengths_row, n_slots):
-    ends = jnp.cumsum(lengths_row)
+    slots = jnp.arange(lengths_row.shape[0])
+    ends = jnp.sum(jnp.where(slots[None, :] <= slots[:, None], lengths_row[None, :], 0), axis=1)
     places = jnp.arange(n_slots, dtype=jnp.int32)
     passed = (places[:, None] >= ends[None, :]).astype(jnp.int32)
     segment = jnp.sum(passed, axis=1)
@@ -104,24 +105,45 @@
 ):
     row_count = tokens.shape[0]
     dp_count = lax.axis_size("dp")
+    fsdp_count = lax.axis_size("fsdp")
     heads_per_group = QUERY_HEADS // KEY_VALUE_HEADS
     score_scale = 1.0 / math.sqrt(HEAD_SIZE)
     n_blocks = row_count // QUERY_BLOCK_ROWS
     segment, position, live_rows, live_total = layout(seq_lengths[0], row_count)
     cosine_table, sine_table = rope_tables(position)
-    attn_local = (
-        lax.all_gather(q_weight, "dp", axis=1, tiled=True),
-        lax.all_gather(k_weight, "dp", axis=1, tiled=True),
-        lax.all_gather(v_weight, "dp", axis=1, tiled=True),
-        lax.all_gather(o_weight, "dp", axis=1, tiled=True),
-    )
-    gain_one, query_full, key_full, value_full, output_full = (
-        lax.all_gather(norm1_gain, "fsdp", axis=0, tiled=True),
-        lax.all_gather(attn_local[0], "fsdp", axis=0, tiled=True),
-        lax.all_gather(attn_local[1], "fsdp", axis=0, tiled=True),
-        lax.all_gather(attn_local[2], "fsdp", axis=0, tiled=True),
-        lax.all_gather(attn_local[3], "fsdp", axis=0, tiled=True),
-    )
+    both = ("fsdp", "dp")
+    q_rows, q_cols = q_weight.shape
+    k_cols = k_weight.shape[1]
+    gains_local = jnp.stack([norm1_gain, norm2_gain], axis=1)
+    pack_qkv = jnp.concatenate([q_weight, k_weight, v_weight, gains_local], axis=1)
+    pack_od = jnp.concatenate([o_weight, down_weight], axis=0)
+    pack_gu = jnp.concatenate([gate_weight, up_weight], axis=1)
+
+    def gather(pack):
+        whole = lax.all_gather(pack, both, axis=0, tiled=False)
+        return whole.reshape((fsdp_count, dp_count) + pack.shape)
+
+    def whole_of(pieces):
+        f, d, r, c = pieces.shape
+        return pieces.transpose(0, 2, 1, 3).reshape(f * r, d * c)
+
+    def chunks_of(whole):
+        r, c = whole.shape
+        return whole.reshape(fsdp_count, r // fsdp_count, dp_count, c // dp_count).transpose(
+            0, 2, 1, 3
+        )
+
+    def scatter(chunks):
+        f, d, r, c = chunks.shape
+        flat = chunks.astype(jnp.bfloat16).reshape(f * d, r, c)
+        return lax.psum_scatter(flat, both, scatter_dimension=0, tiled=False).astype(jnp.float32)
+
+    got_qkv = gather(pack_qkv)
+    query_full = whole_of(got_qkv[..., :q_cols])
+    key_full = whole_of(got_qkv[..., q_cols : q_cols + k_cols])
+    value_full = whole_of(got_qkv[..., q_cols + k_cols : q_cols + 2 * k_cols])
+    gain_one = got_qkv[:, 0, :, q_cols + 2 * k_cols].reshape(-1)
+    gain_two = got_qkv[:, 0, :, q_cols + 2 * k_cols + 1].reshape(-1)
     q_width = query_full.shape[1]
     tokens_wide = tokens.astype(jnp.float32)
     scale_one = norm_scale(tokens_wide)
@@ -178,19 +200,15 @@
         lse_parts.append(lse_block)
     attended = jnp.concatenate(attended_parts, axis=0).astype(jnp.bfloat16)
     row_lse = jnp.concatenate(lse_parts, axis=2)
+    got_od = gather(pack_od)
+    output_full = whole_of(got_od[:, :, :q_rows])
+    down_full = whole_of(got_od[:, :, q_rows:])
     branch_one = jnp.dot(attended, output_full, preferred_element_type=jnp.float32)
     hidden_mid = tokens_wide + branch_one
-    ffn_local = (
-        lax.all_gather(gate_weight, "dp", axis=1, tiled=True),
-        lax.all_gather(up_weight, "dp", axis=1, tiled=True),
-        lax.all_gather(down_weight, "dp", axis=1, tiled=True),
-    )
-    gain_two, gate_full, up_full, down_full = (
-        lax.all_gather(norm2_gain, "fsdp", axis=0, tiled=True),
-        lax.all_gather(ffn_local[0], "fsdp", axis=0, tiled=True),
-        lax.all_gather(ffn_local[1], "fsdp", axis=0, tiled=True),
-        lax.all_gather(ffn_local[2], "fsdp", axis=0, tiled=True),
-    )
+    got_gu = gather(pack_gu)
+    f_cols = gate_weight.shape[1]
+    gate_full = whole_of(got_gu[..., :f_cols])
+    up_full = whole_of(got_gu[..., f_cols:])
     scale_two = norm_scale(hidden_mid)
     normed_two = (hidden_mid * scale_two * gain_two.astype(jnp.float32)[None, :]).astype(
         jnp.bfloat16
@@ -202,36 +220,6 @@
     hidden_ff = (silu_gate * up_proj).astype(jnp.bfloat16)
     branch_two = jnp.dot(hidden_ff, down_full, preferred_element_type=jnp.float32)
     mixed = (live_rows[:, None] * (hidden_mid + branch_two)).astype(jnp.bfloat16)
-    again_local = (
-        lax.all_gather(q_weight, "dp", axis=1, tiled=True),
-        lax.all_gather(k_weight, "dp", axis=1, tiled=True),
-        lax.all_gather(v_weight, "dp", axis=1, tiled=True),
-        lax.all_gather(o_weight, "dp", axis=1, tiled=True),
-        lax.all_gather(gate_weight, "dp", axis=1, tiled=True),
-        lax.all_gather(up_weight, "dp", axis=1, tiled=True),
-        lax.all_gather(down_weight, "dp", axis=1, tiled=True),
-    )
-    (
-        gain_one,
-        query_full,
-        key_full,
-        value_full,
-        output_full,
-        gain_two,
-        gate_full,
-        up_full,
-        down_full,
-    ) = (
-        lax.all_gather(norm1_gain, "fsdp", axis=0, tiled=True),
-        lax.all_gather(again_local[0], "fsdp", axis=0, tiled=True),
-        lax.all_gather(again_local[1], "fsdp", axis=0, tiled=True),
-        lax.all_gather(again_local[2], "fsdp", axis=0, tiled=True),
-        lax.all_gather(again_local[3], "fsdp", axis=0, tiled=True),
-        lax.all_gather(norm2_gain, "fsdp", axis=0, tiled=True),
-        lax.all_gather(again_local[4], "fsdp", axis=0, tiled=True),
-        lax.all_gather(again_local[5], "fsdp", axis=0, tiled=True),
-        lax.all_gather(again_local[6], "fsdp", axis=0, tiled=True),
-    )
     gain_one_wide = gain_one.astype(jnp.float32)
     gain_two_wide = gain_two.astype(jnp.float32)
     grad_mixed = live_rows[:, None] * cotangent.astype(jnp.float32)
@@ -356,62 +344,29 @@
     )
     grad_gain_one = jnp.sum(grad_normed_one * tokens_wide * scale_one, axis=0)
     grad_tokens = grad_mid + norm_back(tokens_wide, scale_one, gain_one_wide, grad_normed_one)
-    row_sums = (
-        lax.psum_scatter(grad_gain_one, "fsdp", scatter_dimension=0, tiled=True),
-        lax.psum_scatter(grad_qw, "fsdp", scatter_dimension=0, tiled=True),
-        lax.psum_scatter(grad_kw, "fsdp", scatter_dimension=0, tiled=True),
-        lax.psum_scatter(grad_vw, "fsdp", scatter_dimension=0, tiled=True),
-        lax.psum_scatter(grad_output, "fsdp", scatter_dimension=0, tiled=True),
-        lax.psum_scatter(grad_gain_two, "fsdp", scatter_dimension=0, tiled=True),
-        lax.psum_scatter(grad_gate, "fsdp", scatter_dimension=0, tiled=True),
-        lax.psum_scatter(grad_up, "fsdp", scatter_dimension=0, tiled=True),
-        lax.psum_scatter(grad_down, "fsdp", scatter_dimension=0, tiled=True),
-    )
-    tiled_one = jnp.broadcast_to(row_sums[0][:, None], (row_sums[0].shape[0], dp_count))
-    tiled_two = jnp.broadcast_to(row_sums[5][:, None], (row_sums[5].shape[0], dp_count))
-    final_sums = (
-        lax.psum_scatter(
-            tiled_one.astype(jnp.bfloat16), "dp", scatter_dimension=1, tiled=True
-        ).astype(jnp.float32),
-        lax.psum_scatter(
-            row_sums[1].astype(jnp.bfloat16), "dp", scatter_dimension=1, tiled=True
-        ).astype(jnp.float32),
-        lax.psum_scatter(
-            row_sums[2].astype(jnp.bfloat16), "dp", scatter_dimension=1, tiled=True
-        ).astype(jnp.float32),
-        lax.psum_scatter(
-            row_sums[3].astype(jnp.bfloat16), "dp", scatter_dimension=1, tiled=True
-        ).astype(jnp.float32),
-        lax.psum_scatter(
-            row_sums[4].astype(jnp.bfloat16), "dp", scatter_dimension=1, tiled=True
-        ).astype(jnp.float32),
-        lax.psum_scatter(
-            tiled_two.astype(jnp.bfloat16), "dp", scatter_dimension=1, tiled=True
-        ).astype(jnp.float32),
-        lax.psum_scatter(
-            row_sums[6].astype(jnp.bfloat16), "dp", scatter_dimension=1, tiled=True
-        ).astype(jnp.float32),
-        lax.psum_scatter(
-            row_sums[7].astype(jnp.bfloat16), "dp", scatter_dimension=1, tiled=True
-        ).astype(jnp.float32),
-        lax.psum_scatter(
-            row_sums[8].astype(jnp.bfloat16), "dp", scatter_dimension=1, tiled=True
-        ).astype(jnp.float32),
-    )
-    gain_sum_one = final_sums[0].reshape(-1)
-    gain_sum_two = final_sums[5].reshape(-1)
+    gain_grads = jnp.stack([grad_gain_one, grad_gain_two], axis=1).reshape(
+        fsdp_count, 1, q_rows, 2
+    )
+    gain_grads = jnp.broadcast_to(gain_grads, (fsdp_count, dp_count, q_rows, 2))
+    sum_gu = scatter(jnp.concatenate([chunks_of(grad_gate), chunks_of(grad_up)], axis=3))
+    sum_od = scatter(jnp.concatenate([chunks_of(grad_output), chunks_of(grad_down)], axis=2))
+    sum_qkv = scatter(
+        jnp.concatenate(
+            [chunks_of(grad_qw), chunks_of(grad_kw), chunks_of(grad_vw), gain_grads], axis=3
+        )
+    )
     return (
         mixed,
         grad_tokens,
-        gain_sum_one,
-        final_sums[1],
-        final_sums[2],
-        final_sums[3],
-        final_sums[4],
-        gain_sum_two,
-        final_sums[6],
-        final_sums[7],
-        final_sums[8],
+        sum_qkv[:, q_cols + 2 * k_cols],
+        sum_qkv[:, :q_cols],
+        sum_qkv[:, q_cols : q_cols + k_cols],
+        sum_qkv[:, q_cols + k_cols : q_cols + 2 * k_cols],
+        sum_od[:q_rows],
+        sum_qkv[:, q_cols + 2 * k_cols + 1],
+        sum_gu[:, :f_cols],
+        sum_gu[:, f_cols:],
+        sum_od[q_rows:],
     )
 
 

time: 1370 us -> 852 us (0.62)
  waiting for transfers between devices: 664 us -> 347 us
  blocking collectives: 292 us -> 0 us
  local copies, waits for them, and re-layouts: 38.1 us -> 148 us
  matrix products: 263 us -> 238 us
    reduce_scatter x7 -> x2, waiting for transfers between devices: 434 us -> 257 us  [scatter(): lax.psum_scatter(flat, both, scatter_dimension=0, tiled=False)]
    unnamed x3 -> x0, blocking collectives: 175 us -> none
    all_gather x9 -> x0, blocking collectives: 117 us -> none  [the longest x1 33.5 us: shards(): lax.all_gather(attn_local[1], 'fsdp', axis=0, tiled=True)]
    unnamed x22 -> x7, waiting for transfers between devices: 113 us -> 0.1 us
    reshape x0 -> x10, local copies, waits for them, and re-layouts: none -> 65.5 us  [the longest x5 43.8 us: chunks_of(): whole.reshape(fsdp_count, r // fsdp_count, dp_count, c // dp_count)]
    all_gather x5 -> x3, waiting for transfers between devices: 117 us -> 90.4 us  [gather(): whole = lax.all_gather(pack, both, axis=0, tiled=False)]
    transpose x0 -> x8, local copies, waits for them, and re-layouts: none -> 21 us  [the longest x4 15.3 us: chunks_of(): whole.reshape(fsdp_count, r // fsdp_count, dp_count, c // dp_count)]
    concatenate x2 -> x5, other arithmetic: 0.24 us -> 19.5 us  [the longest x1 6.99 us: shards(): jnp.concatenate([chunks_of(grad_gate), chunks_of(grad_up)], axis=3)]
  transfers between devices with their start and end apart: 17 -> 6, of which waited for: 11 -> 4; matrix products, arithmetic and copies ran while one was open for 24% -> 30% of each run, Pallas kernels for 0% -> 0%
where the time goes in v1:
time: 852 us; the launch traced here: 846 us
  waiting for transfers between devices  347 us (41%)
  matrix products  238 us (28%)
  local copies, waits for them, and re-layouts  148 us (17%)
  other arithmetic  97.6 us (11%)
  between operations  15.3 us (2%)
    reduce_scatter x2, waiting for transfers between devices, scatter(): lax.psum_scatter(flat, both, scatter_dimension=0, tiled=False)  257 us
    all_gather x3, waiting for transfers between devices, gather(): whole = lax.all_gather(pack, both, axis=0, tiled=False)  90.4 us
    reshape x5, local copies, waits for them, and re-layouts, chunks_of(): whole.reshape(fsdp_count, r // fsdp_count, dp_count, c // dp_count)  43.8 us
    convert_element_type x2, other arithmetic, backward_block(): grad_scores = (attn_probs * (grad_probs - row_dot)).astype(jnp.bfloat16)  34.8 us
    unnamed x145, local copies, waits for them, and re-layouts  33.9 us
    dot_general x2, matrix products, backward_block(): jnp.einsum('tngd,und->ngtu', block_gradient, value_row_slice[:ending_row]...  31.2 us
    reshape x5, local copies, waits for them, and re-layouts, whole_of(): return pieces.transpose(0, 2, 1, 3).reshape(f * r, d * c)  21.8 us
    dot_general x2, matrix products, block_scores(): jnp.einsum('tngd,und->ngtu', query_block_rows, key_rows, preferred_elemen...  21.4 us
  transfers between devices with their start and end apart: 6, of which 4 were waited for; matrix products, arithmetic and copies ran while one was open for 30% of the time, Pallas kernels for 0%

profile of v1, /device:TPU:0, one launch (start us, length us, event | category | flops | bytes accessed | tf_op | source)
XLA Modules:
  0.0 846.1 jit_solution(7790604132336636490)
XLA Ops:
  8.2 4.6 concatenate.70
  24.2 50.9 %all-gather.12.cloned.1.call-done = bf16[32,120,402]{1,2,0:T(8,128)(2,1)} async-done(((bf16[1,120,402]{1,2,0:T(8,128)(2,1)}), bf16[32,120,402]{1,2,0:T(8,128)(2,1)}) %all-gather.12.cloned.1.call-update) | async-done | bytes 3087376 | tf_op jit(solution)/shard_map/all_gather | solution.py:123
  98.3 7.0 fusion.83
  105.3 7.8 fusion.12
  113.8 14.4 %fusion.82 = (f32[5,3,512]{2,1,0:T(4,128)S(1)}, f32[5,3,512,1024]{2,3,1,0:T(8,128)}) fusion(bf16[512,5,3,64]{0,3,2,1:T(8,128)(2,1)S(1)} %bitcast.293, bf16[1024,5,32]{0,2,1:T(8,128)(2,1)S(1)} %get-tuple-element.156, bf16[1024,5,32]{0,2,1:T(8,128)(2,1)S(1)} %get-tuple-element.155, pred[512,1024]{0,1:T(8,128)(4,1)S(1)} %fusion.29), kind=kOutput, calls=%fused_computation.169 | convolution fusion | flops 1031528960 | bytes 33650688 | tf_op jit(solution)/shard_map/tngd,und->ngtu/dot_general | solution.py:81
  128.2 13.2 %fusion.3 = f32[5,3,512]{2,1,0:T(4,128)S(1)} fusion(f32[5,3,512,1024]{2,3,1,0:T(8,128)} %get-tuple-element.172, f32[5,3,512]{2,1,0:T(4,128)S(1)} %get-tuple-element.171), kind=kLoop, calls=%fused_computation.9 | loop fusion | flops 15720960 | bytes 31518720 | tf_op jit(solution)/shard_map/reduce_sum | solution.py:185
  145.0 14.6 %fusion.39 = bf16[5,64,3,512]{3,1,2,0:T(8,128)(2,1)} fusion(bf16[1024,5,64,1]{0,2,3,1:T(8,128)(2,1)S(1)} %bitcast.329, f32[5,3,512,1024]{2,3,1,0:T(8,128)} %get-tuple-element.172, f32[5,3,512]{2,1,0:T(4,128)S(1)} %fusion.3, f32[5,3,512]{2,1,0:T(4,128)S(1)} %get-tuple-element.171), kind=kOutput, calls=%fused_computation.91 | convolution fusion | flops 1030717440 | bytes 33157120 | tf_op jit(solution)/shard_map/ngtu,und->tngd/dot_general | solution.py:187
  165.5 6.3 copy.179
  171.8 10.0 %reshape.533 = bf16[2560,960]{1,0:T(8,128)(2,1)} reshape(bf16[8,320,4,240]{3,2,1,0:T(4,128)(2,1)} %bitcast.281) | data formatting | bytes 9830400 | tf_op jit(solution)/shard_map/reshape | solution.py:128
  181.8 4.2 copy.166
  186.0 4.4 reshape.529
  190.4 4.1 multiply_reduce_fusion.2
  196.8 39.5 %all-gather.10.cloned.1.call-done = bf16[3840,1280]{1,0:T(8,128)(2,1)} async-done(((bf16[120,1280]{1,0:T(8,128)(2,1)}), bf16[3840,1280]{1,0:T(8,128)(2,1)}) %all-gather.10.cloned.1.call-update) | async-done | bytes 9830416 | tf_op jit(solution)/shard_map/all_gather | solution.py:123
  236.3 6.9 fusion.76
  243.2 4.3 copy.170
  253.3 8.8 %fusion.85 = f32[1024,2560]{1,0:T(8,128)} fusion(bf16[1024,960]{0,1:T(8,128)(2,1)S(1)} %multiply_convert_fusion.4, bf16[960,2560]{1,0:T(8,128)(2,1)S(1)} %bitcast.311), kind=kOutput, calls=%fused_computation.172 | convolution fusion | flops 5033164800 | bytes 17367040 | tf_op jit(solution)/shard_map/dot_general | solution.py:217
  262.1 10.0 %fusion.84 = f32[1024,2560]{1,0:T(8,128)} fusion(bf16[1024,960]{0,1:T(8,128)(2,1)} %copy-done.39, bf16[960,2560]{1,0:T(8,128)(2,1)S(1)} %bitcast.310), kind=kOutput, calls=%fused_computation.171 | convolution fusion | flops 5033164800 | bytes 17367040 | tf_op jit(solution)/shard_map/dot_general | solution.py:216
  272.1 18.9 %multiply_convert_fusion = (bf16[1024,2560]{1,0:T(8,128)(2,1)}, bf16[1024,2560]{1,0:T(8,128)(2,1)}, bf16[1024,2560]{1,0:T(8,128)(2,1)}) fusion(f32[1024,2560]{1,0:T(8,128)} %fusion.84, f32[1024,2560]{1,0:T(8,128)} %fusion.85, bf16[2560,960]{1,0:T(8,128)(2,1)} %reshape.533, bf16[1024,960]{0,1:T(8,128)(2,1)S(1)} %copy-done.33, f32[1024]{0:T(1024)S(1)} %copy-done.52), kind=kOutput, calls=%fused_computation.25 | convolution fusion | flops 5075435520 | bytes 43585536 | tf_op jit(solution)/shard_map/td,fd->tf/dot_general | solution.py:228
  291.0 9.0 %fusion.86 = f32[1024,960]{0,1:T(8,128)S(1)} fusion(bf16[1024,2560]{1,0:T(8,128)(2,1)} %get-tuple-element.137, bf16[960,2560]{1,0:T(8,128)(2,1)} %bitcast.307), kind=kOutput, calls=%fused_computation.173 | convolution fusion | flops 5033164800 | bytes 14090240 | tf_op jit(solution)/shard_map/tf,df->td/dot_general | solution.py:237
  300.0 5.9 multiply_reduce_fusion
  317.1 7.3 fusion.7
  324.4 7.9 fusion.9
  337.2 23.9 %fusion = (f32[5,3,512]{2,1,0:T(4,128)S(1)}, f32[5,1024,512,3]{2,1,3,0:T(8,128)}) fusion(f32[5,3,512,1024]{2,3,1,0:T(8,128)} %get-tuple-element.172, f32[5,3,512]{2,1,0:T(4,128)S(1)} %copy-done.45, bf16[1024,5,64,1]{0,2,3,1:T(8,128)(2,1)} %bitcast.330, bf16[512,5,3,64]{0,3,2,1:T(8,128)(2,1)S(1)} %bitcast.295), kind=kOutput, calls=%fused_computation.2 | convolution fusion | flops 1030218240 | bytes 64614400 | tf_op jit(solution)/shard_map/tngd,und->ngtu/dot_general | solution.py:274
  361.1 13.5 %fusion.46 = bf16[1024,5,64]{0,2,1:T(8,128)(2,1)} fusion(bf16[512,5,3,64]{0,3,2,1:T(8,128)(2,1)S(1)} %bitcast.296, f32[5,3,512,1024]{2,3,1,0:T(8,128)} %get-tuple-element.172, f32[5,3,512]{2,1,0:T(4,128)S(1)} %copy-done.45, f32[512,5,64]{0,2,1:T(8,128)S(1)} %copy-done.29), kind=kOutput, calls=%fused_computation.95 | convolution fusion | flops 1023016960 | bytes 33781760 | tf_op jit(solution)/shard_map/ngtu,tngd->und/dot_general | solution.py:300
  374.6 26.9 %fusion.2 = bf16[5,3,512,1024]{2,3,1,0:T(8,128)(2,1)} fusion(f32[5,1024,512,3]{2,1,3,0:T(8,128)} %get-tuple-element.179, f32[5,3,512,1024]{2,3,1,0:T(8,128)} %get-tuple-element.172, f32[5,3,512]{2,1,0:T(4,128)S(1)} %get-tuple-element.178, f32[5,3,512]{2,1,0:T(4,128)S(1)} %copy-done.45), kind=kLoop, calls=%fused_computation.4 | loop fusion | flops 31457280 | bytes 78704640 | tf_op jit(solution)/shard_map/convert_element_type | solution.py:281
  401.5 9.6 %convolution_multiply_fusion = f32[5,64,3,512]{3,1,2,0:T(8,128)} fusion(bf16[5,3,512,1024]{2,3,1,0:T(8,128)(2,1)} %fusion.2, bf16[1024,5,32]{0,2,1:T(8,128)(2,1)S(1)} %copy-done.14, bf16[1024,5,32]{0,2,1:T(8,128)(2,1)S(1)} %copy-done.11), kind=kOutput, calls=%fused_computation.88 | convolution fusion | flops 1008435200 | bytes 18350080 | tf_op jit(solution)/shard_map/ngtu,und->tngd/dot_general | solution.py:283
  411.2 10.4 %fusion.51 = f32[1024,5,64]{0,2,1:T(8,128)S(1)} fusion(bf16[512,5,3,64]{0,3,2,1:T(8,128)(2,1)S(1)} %bitcast.294, bf16[5,3,512,1024]{2,3,1,0:T(8,128)(2,1)} %fusion.2, f32[512,5,64]{0,2,1:T(8,128)} %fusion.56), kind=kOutput, calls=%fused_computation.101 | convolution fusion | flops 1007288320 | bytes 18677760 | tf_op jit(solution)/shard_map/ngtu,tngd->und/dot_general | solution.py:292
  421.9 3.6 convolution_convert_fusion.7
  428.2 3.5 convolution_convert_fusion.4
  431.8 4.7 copy.141
  436.5 3.9 fusion.87
  442.3 3.9 fusion.27
  449.8 9.9 %convolution_convert_fusion.2 = bf16[960,2560]{1,0:T(8,128)(2,1)} fusion(bf16[1024,960]{0,1:T(8,128)(2,1)} %copy-done.39, bf16[1024,2560]{1,0:T(8,128)(2,1)} %get-tuple-element.137), kind=kOutput, calls=%fused_computation.43 | convolution fusion | flops 5035622400 | bytes 12124160 | tf_op jit(solution)/shard_map/td,tf->df/dot_general | solution.py:233
  459.7 9.4 %reshape.541 = bf16[8,120,4,640]{3,2,1,0:T(4,128)(2,1)} reshape(bf16[960,2560]{1,0:T(8,128)(2,1)} %convolution_convert_fusion.2) | data formatting | bytes 9830400 | tf_op jit(solution)/shard_map/reshape | solution.py:132
  469.1 5.6 copy.145
  474.7 9.6 %convolution_convert_fusion.1 = bf16[960,2560]{1,0:T(8,128)(2,1)} fusion(bf16[1024,960]{0,1:T(8,128)(2,1)S(1)} %copy-done.40, bf16[1024,2560]{1,0:T(8,128)(2,1)} %get-tuple-element.136), kind=kOutput, calls=%fused_computation.42 | convolution fusion | flops 5035622400 | bytes 12124160 | tf_op jit(solution)/shard_map/td,tf->df/dot_general | solution.py:236
  484.2 9.4 %reshape.542 = bf16[8,120,4,640]{3,2,1,0:T(4,128)(2,1)} reshape(bf16[960,2560]{1,0:T(8,128)(2,1)} %convolution_convert_fusion.1) | data formatting | bytes 9830400 | tf_op jit(solution)/shard_map/reshape | solution.py:132
  496.7 7.0 pad_maximum_fusion
  504.9 6.0 convolution_convert_fusion.3
  510.9 6.2 reshape.539
  520.4 9.5 %convolution_convert_fusion = bf16[2560,960]{0,1:T(8,128)(2,1)} fusion(bf16[1024,2560]{1,0:T(8,128)(2,1)} %get-tuple-element.138, bf16[1024,960]{0,1:T(8,128)(2,1)S(1)} %copy-done.34, f32[1024]{0:T(1024)S(1)} %copy-done.53), kind=kOutput, calls=%fused_computation.41 | convolution fusion | flops 5038571520 | bytes 12128256 | tf_op jit(solution)/shard_map/tf,td->fd/dot_general | solution.py:227
  529.9 10.0 %reshape.570 = bf16[8,320,4,240]{1,0,3,2:T(8,128)(2,1)} reshape(bf16[2560,960]{0,1:T(8,128)(2,1)} %convolution_convert_fusion) | data formatting | bytes 9830400 | tf_op jit(solution)/shard_map/reshape | solution.py:132
  539.8 8.7 %copy.165 = bf16[8,320,4,240]{3,2,1,0:T(4,128)(2,1)} copy(bf16[8,320,4,240]{1,0,3,2:T(8,128)(2,1)} %reshape.570) | data formatting | bytes 9830400 | tf_op jit(solution)/shard_map/reshape | solution.py:132
  552.0 5.8 pad_maximum_fusion.1
  558.5 6.7 fusion.24
  565.2 10.1 %multiply_convert_fusion.3 = bf16[1024,960]{0,1:T(8,128)(2,1)} fusion(f32[1024,960]{0,1:T(8,128)S(1)} %copy-done.4, f32[1024]{0:T(1024)S(1)} %copy-done.53, bf16[1024,2560]{1,0:T(8,128)(2,1)} %get-tuple-element.138, bf16[2560,960]{1,0:T(8,128)(2,1)} %reshape.533), kind=kOutput, calls=%fused_computation.63 | convolution fusion | flops 5036113920 | bytes 16060416 | tf_op jit(solution)/shard_map/dot_general | solution.py:221
  578.1 110.4 %reduce-scatter.8.cloned.1.call-done = bf16[1,120,1280]{2,1,0:T(8,128)(2,1)} async-done(((bf16[32,120,1280]{2,1,0:T(8,128)(2,1)}), bf16[1,120,1280]{2,1,0:T(8,128)(2,1)}) %reduce-scatter.8.cloned.1.call-update) | async-done | bytes 307216 | tf_op jit(solution)/shard_map/reduce_scatter | solution.py:139
  690.4 146.2 %reduce-scatter.6.cloned.1.call-done = bf16[1,440,240]{2,1,0:T(8,128)(2,1)} async-done(((bf16[32,440,240]{2,1,0:T(8,128)(2,1)}), bf16[1,440,240]{2,1,0:T(8,128)(2,1)}) %reduce-scatter.6.cloned.1.call-update) | async-done | bytes 211216 | tf_op jit(solution)/shard_map/reduce_scatter | solution.py:139
  (230 shorter events, 96.4 us)
Async XLA Ops:
  7.2 68.0 %all-gather.12.cloned.1.call-start = ((), (), s32[]{:S(2)}) async-start(), calls=%async_computation.7 | async-start | bytes 3446784 | tf_op jit(solution)/shard_map/all_gather | solution.py:123
  12.8 146.8 %all-gather.8.cloned.1.call-start = ((), (), s32[]{:S(2)}) async-start(), calls=%async_computation.5 | async-start | bytes 7434240 | tf_op jit(solution)/shard_map/all_gather | solution.py:123
  14.5 221.8 %all-gather.10.cloned.1.call-start = ((), (), s32[]{:S(2)}) async-start(), calls=%async_computation.6 | async-start | bytes 10137600 | tf_op jit(solution)/shard_map/all_gather | solution.py:123
  16.3 559.0 %reduce-scatter.10.cloned.1.call-start = ((), (), s32[]{:S(2)}) async-start(), calls=%async_computation.8 | async-start | bytes 3446784
  22.3 68.3 %copy-start.48 = (f32[1024]{0:T(1024)}, f32[1024]{0:T(1024)S(1)}, u32[]{:S(2)}) copy-start(f32[1024]{0:T(1024)S(1)} %get-tuple-element.166) | copy-start | bytes 12292
  23.8 74.2 %copy-start.20 = (f32[1024,32]{0,1:T(8,128)}, f32[1024,32]{0,1:T(8,128)S(1)}, u32[]{:S(2)}) copy-start(f32[1024,32]{0,1:T(8,128)S(1)} %get-tuple-element.163) | copy-start | bytes 393220
  23.8 74.2 %copy-start.22 = (f32[1024,32]{0,1:T(8,128)}, f32[1024,32]{0,1:T(8,128)S(1)}, u32[]{:S(2)}) copy-start(f32[1024,32]{0,1:T(8,128)S(1)} %get-tuple-element.164) | copy-start | bytes 393220
  76.1 14.4 %copy-start.50 = (f32[960]{0:T(1024)}, f32[960]{0:T(1024)S(1)}, u32[]{:S(2)}) copy-start(f32[960]{0:T(1024)S(1)} %reshape.543) | copy-start | bytes 11524
  82.5 8.1 copy-start
  91.1 5.8 copy-start.37
  92.0 53.0 %copy-start.43 = (bf16[1024,320]{0,1:T(8,128)(2,1)}, bf16[1024,320]{0,1:T(8,128)(2,1)S(1)}, u32[]{:S(2)}) copy-start(bf16[1024,320]{0,1:T(8,128)(2,1)S(1)} %convolution_convert_fusion.6) | copy-start | bytes 1966084
  92.0 50.0 %copy-start.31 = (bf16[512,320]{0,1:T(8,128)(2,1)}, bf16[512,320]{0,1:T(8,128)(2,1)S(1)}, u32[]{:S(2)}) copy-start(bf16[512,320]{0,1:T(8,128)(2,1)S(1)} %slice.244) | copy-start | bytes 983044
  96.9 16.9 %copy-start.8 = (bf16[512,15,64]{0,2,1:T(8,128)(2,1)}, bf16[512,15,64]{0,2,1:T(8,128)(2,1)S(1)}, u32[]{:S(2)}) copy-start(bf16[512,15,64]{0,2,1:T(8,128)(2,1)S(1)} %get-tuple-element.152) | copy-start | bytes 2949124
  98.2 15.6 %copy-start.10 = (bf16[1024,5,32]{0,2,1:T(8,128)(2,1)}, bf16[1024,5,32]{0,2,1:T(8,128)(2,1)S(1)}, u32[]{:S(2)}) copy-start(bf16[1024,5,32]{0,2,1:T(8,128)(2,1)S(1)} %get-tuple-element.155) | copy-start | bytes 983044
  98.2 15.6 %copy-start.12 = (bf16[1024,5,32]{0,2,1:T(8,128)(2,1)}, bf16[1024,5,32]{0,2,1:T(8,128)(2,1)S(1)}, u32[]{:S(2)}) copy-start(bf16[1024,5,32]{0,2,1:T(8,128)(2,1)S(1)} %get-tuple-element.156) | copy-start | bytes 983044
  113.8 28.2 %slice-start = ((s8[15728640]{0:T(1024)(128)(4,1)}), s8[4194304]{0:T(1024)(128)(4,1)S(1)}, s32[]{:S(2)}) async-start(s8[15728640]{0:T(1024)(128)(4,1)} %bitcast.276), calls=%async_computation.9 | async-start | bytes 8388608
  113.8 28.2 %slice-start.1 = ((s8[15728640]{0:T(1024)(128)(4,1)}), s8[4194304]{0:T(1024)(128)(4,1)S(1)}, s32[]{:S(2)}) async-start(s8[15728640]{0:T(1024)(128)(4,1)} %bitcast.276), calls=%async_computation.10 | async-start | bytes 8388608
  113.8 28.2 %slice-start.2 = ((s8[15728640]{0:T(1024)(128)(4,1)}), s8[3145728]{0:T(1024)(128)(4,1)S(1)}, s32[]{:S(2)}) async-start(s8[15728640]{0:T(1024)(128)(4,1)} %bitcast.276), calls=%async_computation.11 | async-start | bytes 6291456
  128.2 13.8 %slice-start.3 = ((s8[15728640]{0:T(1024)(128)(4,1)}), s8[4194304]{0:T(1024)(128)(4,1)S(1)}, s32[]{:S(2)}) async-start(s8[15728640]{0:T(1024)(128)(4,1)} %bitcast.276), calls=%async_computation.12 | async-start | bytes 8388608
  145.0 45.3 %copy-start.55 = (bf16[5,64,3,512]{3,1,2,0:T(8,128)(2,1)}, bf16[5,64,3,512]{3,1,2,0:T(8,128)(2,1)S(1)}, u32[]{:S(2)}) copy-start(bf16[5,64,3,512]{3,1,2,0:T(8,128)(2,1)S(1)} %fusion.38) | copy-start | bytes 2949124
  196.8 56.5 %copy-start.39 = (bf16[1024,960]{0,1:T(8,128)(2,1)}, bf16[1024,960]{0,1:T(8,128)(2,1)S(1)}, u32[]{:S(2)}) copy-start(bf16[1024,960]{0,1:T(8,128)(2,1)S(1)} %multiply_convert_fusion.4) | copy-start | bytes 5898244
  252.4 9.7 %slice-start.8 = ((s8[4915200]{0:T(1024)(128)(4,1)}), s8[720896]{0:T(1024)(128)(4,1)S(1)}, s32[]{:S(2)}) async-start(s8[4915200]{0:T(1024)(128)(4,1)} %bitcast.308), calls=%async_computation.17 | async-start | bytes 1441792
  253.2 8.9 %copy-start.18 = (bf16[120,8,4,640]{3,1,2,0:T(8,128)(2,1)}, bf16[120,8,4,640]{3,1,2,0:T(8,128)(2,1)S(1)}, u32[]{:S(2)}) copy-start(bf16[120,8,4,640]{3,1,2,0:T(8,128)(2,1)S(1)} %copy.174) | copy-start | bytes 14745604
  253.2 8.8 %slice-start.9 = ((s8[4915200]{0:T(1024)(128)(4,1)}), s8[4194304]{0:T(1024)(128)(4,1)S(1)}, s32[]{:S(2)}) async-start(s8[4915200]{0:T(1024)(128)(4,1)} %bitcast.308), calls=%async_computation.18 | async-start | bytes 8388608
  262.1 10.0 %copy-start.33 = (bf16[1024,960]{0,1:T(8,128)(2,1)S(1)}, bf16[1024,960]{0,1:T(8,128)(2,1)}, u32[]{:S(2)}) copy-start(bf16[1024,960]{0,1:T(8,128)(2,1)} %param.35) | copy-start | bytes 5898244
  262.1 10.0 %copy-start.52 = (f32[1024]{0:T(1024)S(1)}, f32[1024]{0:T(1024)}, u32[]{:S(2)}) copy-start(f32[1024]{0:T(1024)} %fusion.69) | copy-start | bytes 12292
  291.0 9.0 %copy-start.3 = (f32[1024,960]{0,1:T(8,128)S(1)}, f32[1024,960]{0,1:T(8,128)}, u32[]{:S(2)}) copy-start(f32[1024,960]{0,1:T(8,128)} %copy-done.2) | copy-start | bytes 11796484
  291.0 9.0 %copy-start.19 = (bf16[120,8,4,640]{3,1,2,0:T(8,128)(2,1)S(1)}, bf16[120,8,4,640]{3,1,2,0:T(8,128)(2,1)}, u32[]{:S(2)}) copy-start(bf16[120,8,4,640]{3,1,2,0:T(8,128)(2,1)} %copy-done.18) | copy-start | bytes 14745604
  291.0 9.0 %copy-start.57 = (bf16[1024,2560]{1,0:T(8,128)(2,1)S(1)}, bf16[1024,2560]{1,0:T(8,128)(2,1)}, u32[]{:S(2)}) copy-start(bf16[1024,2560]{1,0:T(8,128)(2,1)} %get-tuple-element.136) | copy-start | bytes 15728644
  306.0 5.7 slice-start.4
  306.0 5.7 slice-start.5
  309.2 4.5 slice-start.7
  324.4 7.9 copy-start.7
  337.2 23.9 %copy-start.29 = (f32[512,5,64]{0,2,1:T(8,128)S(1)}, f32[512,5,64]{0,2,1:T(8,128)}, u32[]{:S(2)}) copy-start(f32[512,5,64]{0,2,1:T(8,128)} %fusion.52) | copy-start | bytes 1966084
  374.6 26.9 %copy-start.14 = (bf16[1024,5,32]{0,2,1:T(8,128)(2,1)S(1)}, bf16[1024,5,32]{0,2,1:T(8,128)(2,1)}, u32[]{:S(2)}) copy-start(bf16[1024,5,32]{0,2,1:T(8,128)(2,1)} %copy-done.12) | copy-start | bytes 983044
  401.5 9.6 %copy-start.9 = (bf16[512,15,64]{0,2,1:T(8,128)(2,1)S(1)}, bf16[512,15,64]{0,2,1:T(8,128)(2,1)}, u32[]{:S(2)}) copy-start(bf16[512,15,64]{0,2,1:T(8,128)(2,1)} %copy-done.8) | copy-start | bytes 2949124
  411.2 10.5 %copy-start.21 = (f32[1024,32]{0,1:T(8,128)S(1)}, f32[1024,32]{0,1:T(8,128)}, u32[]{:S(2)}) copy-start(f32[1024,32]{0,1:T(8,128)} %copy-done.20) | copy-start | bytes 393220
  411.2 10.5 %copy-start.23 = (f32[1024,32]{0,1:T(8,128)S(1)}, f32[1024,32]{0,1:T(8,128)}, u32[]{:S(2)}) copy-start(f32[1024,32]{0,1:T(8,128)} %copy-done.22) | copy-start | bytes 393220
  421.9 5.5 copy-start.15
  431.8 4.7 copy-start.36
  436.5 3.9 copy-start.17
  442.3 4.1 copy-start.46
  442.3 4.1 copy-start.47
  449.7 238.8 %reduce-scatter.8.cloned.1.call-start = ((), (), s32[]{:S(2)}) async-start(), calls=%async_computation.4 | async-start | bytes 10137600 | tf_op jit(solution)/shard_map/reduce_scatter | solution.py:139
  469.1 5.6 copy-start.40
  503.7 332.9 %reduce-scatter.6.cloned.1.call-start = ((), (), s32[]{:S(2)}) async-start(), calls=%async_computation.3 | async-start | bytes 7434240 | tf_op jit(solution)/shard_map/reduce_scatter | solution.py:139
  510.9 9.5 %copy-start.53 = (f32[1024]{0:T(1024)S(1)}, f32[1024]{0:T(1024)}, u32[]{:S(2)}) copy-start(f32[1024]{0:T(1024)} %fusion.69) | copy-start | bytes 12292
  558.5 6.7 copy-start.4
  (26 other events, 60.0 us)
Sparse Core Ops, SparseCore 0:
  12.9 62.2 all-gather.11
  78.6 71.7 all-gather.7
  153.9 82.3 all-gather.9
  449.8 94.9 reduce-scatter.9
  551.7 136.8 reduce-scatter.7
  690.7 145.8 reduce-scatter.5

commit v2 on v1

v2 whole, which is shorter than its diff:
```python
import functools
import math
import jax
import jax.numpy as jnp
from jax import lax
from jax.experimental import pallas as pl
from jax.experimental.pallas import tpu as pltpu
from jax.sharding import Mesh
from jax.sharding import PartitionSpec as P

QUERY_HEADS = 15
KEY_VALUE_HEADS = 5
HEAD_SIZE = 64
QUERY_BLOCK = 256
ROW_BLOCK = 256
SEGMENT_ROWS = 16
epsilon = 1e-05
rope_base = 100000.0
masked_fill = -1e30


def product(left, right):
    return jnp.dot(left, right, preferred_element_type=jnp.float32)


def stacked_split(row):
    high = row.astype(jnp.bfloat16).astype(jnp.float32)
    middle = (row - high).astype(jnp.bfloat16).astype(jnp.float32)
    low = row - high - middle
    place = lax.broadcasted_iota(jnp.int32, (SEGMENT_ROWS, row.shape[1]), 0)
    return jnp.where(
        place == 0, high, jnp.where(place == 1, middle, jnp.where(place == 2, low, 0.0))
    ).astype(jnp.bfloat16)


def causal(block):
    key_place = lax.broadcasted_iota(jnp.int32, (block, block), 0)
    query_place = lax.broadcasted_iota(jnp.int32, (block, block), 1)
    return key_place <= query_place


def attention_forward_kernel(onehot_ref, penalty_ref, q_ref, k_ref, v_ref, o_ref, lse_ref, key_rows):
    rows = q_ref.shape[1]
    block = min(QUERY_BLOCK, rows)
    filler = jnp.zeros((HEAD_SIZE - SEGMENT_ROWS, rows), jnp.bfloat16)
    key_rows[...] = jnp.concatenate([k_ref[...], onehot_ref[...], filler], axis=0).T
    allowed = causal(block)
    lse_ref[...] = jnp.zeros_like(lse_ref)
    for i in range(rows // block):
        start, stop = i * block, (i + 1) * block
        for h in range(q_ref.shape[0] // HEAD_SIZE):
            q_side = jnp.concatenate(
                [
                    q_ref[h * HEAD_SIZE : (h + 1) * HEAD_SIZE, start:stop],
                    penalty_ref[:, start:stop],
                    filler[:, :block],
                ],
                axis=0,
            )
            near = jnp.where(allowed, product(key_rows[start:stop], q_side), masked_fill)
            peak = jnp.max(near, axis=0, keepdims=True)
            if i:
                far = product(key_rows[:start], q_side)
                peak = jnp.maximum(peak, jnp.max(far, axis=0, keepdims=True))
            near = jnp.exp(near - peak)
            total = jnp.sum(near, axis=0, keepdims=True)
            out = product(v_ref[:, start:stop], near.astype(jnp.bfloat16))
            if i:
                far = jnp.exp(far - peak)
                total = total + jnp.sum(far, axis=0, keepdims=True)
                out = out + product(v_ref[:, :start], far.astype(jnp.bfloat16))
            o_ref[h * HEAD_SIZE : (h + 1) * HEAD_SIZE, start:stop] = (out / total).astype(
                jnp.bfloat16
            )
            lse_ref[0, h : h + 1, start:stop] = peak + jnp.log(total)


def attention_backward_kernel(
    onehot_ref, penalty_ref, cos_ref, sin_ref, q_ref, k_ref, v_ref, o_ref, do_ref, lse_ref,
    dq_ref, dk_ref, dv_ref, key_rows, value_rows, pair_rows, weights, sums,
):
    rows = q_ref.shape[1]
    block = min(QUERY_BLOCK, rows)
    heads = q_ref.shape[0] // HEAD_SIZE
    half = HEAD_SIZE // 2
    scale = 1.0 / math.sqrt(HEAD_SIZE)
    ones = jnp.ones((SEGMENT_ROWS, rows), jnp.bfloat16)
    zeros = jnp.zeros((HEAD_SIZE, rows), jnp.bfloat16)
    short = zeros[: HEAD_SIZE - 2 * SEGMENT_ROWS]
    long = zeros[: HEAD_SIZE - SEGMENT_ROWS]
    key_rows[...] = jnp.concatenate([k_ref[...], onehot_ref[...], ones, short], axis=0).T
    value_rows[...] = jnp.concatenate([v_ref[...], ones, long], axis=0).T
    count = rows // block
    for h in range(heads):
        q_rows = jnp.concatenate([q_ref[h * HEAD_SIZE : (h + 1) * HEAD_SIZE], zeros], axis=0).T
        do_rows = jnp.concatenate([zeros, do_ref[h * HEAD_SIZE : (h + 1) * HEAD_SIZE]], axis=0).T
        for i in range(count):
            pair_rows[i, 2 * h * block : (2 * h + 1) * block] = q_rows[i * block : (i + 1) * block]
            pair_rows[i, (2 * h + 1) * block : (2 * h + 2) * block] = do_rows[
                i * block : (i + 1) * block
            ]
    allowed = causal(block)

    def back(w):
        return w[:half], w[half:]

    for i in reversed(range(count)):
        start, stop = i * block, (i + 1) * block
        cos, sin = cos_ref[:, start:stop], sin_ref[:, start:stop]
        for h in range(heads):
            own = slice(h * HEAD_SIZE, (h + 1) * HEAD_SIZE)
            do = do_ref[own, start:stop]
            delta = jnp.sum(
                do.astype(jnp.float32) * o_ref[own, start:stop].astype(jnp.float32),
                axis=0, keepdims=True,
            )
            q_side = jnp.concatenate(
                [
                    q_ref[own, start:stop], penalty_ref[:, start:stop],
                    stacked_split(-lse_ref[0, h : h + 1, start:stop]), short[:, :block],
                ],
                axis=0,
            )
            do_side = jnp.concatenate([do, stacked_split(-delta), long[:, :block]], axis=0)
            left, middle, right = 2 * h * block, (2 * h + 1) * block, (2 * h + 2) * block
            probs = jnp.exp(
                jnp.where(allowed, product(key_rows[start:stop], q_side), masked_fill)
            )
            grads = (probs * product(value_rows[start:stop], do_side)).astype(jnp.bfloat16)
            weights[start:stop, left:middle] = grads
            weights[start:stop, middle:right] = probs.astype(jnp.bfloat16)
            dq = product(k_ref[:, start:stop], grads)
            if i:
                probs = jnp.exp(product(key_rows[:start], q_side))
                grads = (probs * product(value_rows[:start], do_side)).astype(jnp.bfloat16)
                weights[:start, left:middle] = grads
                weights[:start, middle:right] = probs.astype(jnp.bfloat16)
                dq = dq + product(k_ref[:, :start], grads)
            w1, w2 = back(dq * scale)
            dq_ref[h * HEAD_SIZE : h * HEAD_SIZE + half, start:stop] = (
                w1 * cos + w2 * sin
            ).astype(jnp.bfloat16)
            dq_ref[h * HEAD_SIZE + half : (h + 1) * HEAD_SIZE, start:stop] = (
                w2 * cos - w1 * sin
            ).astype(jnp.bfloat16)
        part = product(weights[:stop], pair_rows[i])
        if i == count - 1:
            sums[...] = part
        else:
            sums[:stop] = sums[:stop] + part
    both = sums[...].T
    w1, w2 = back(both[:HEAD_SIZE])
    cos, sin = cos_ref[...], sin_ref[...]
    dk_ref[:half] = (w1 * cos + w2 * sin).astype(jnp.bfloat16)
    dk_ref[half:] = (w2 * cos - w1 * sin).astype(jnp.bfloat16)
    dv_ref[...] = both[HEAD_SIZE:].astype(jnp.bfloat16)


def attention_specs(rows, low=0):
    group = QUERY_HEADS // KEY_VALUE_HEADS * HEAD_SIZE
    whole = pl.BlockSpec((SEGMENT_ROWS, rows), lambda g: (0, 0))
    table = pl.BlockSpec((HEAD_SIZE // 2, rows), lambda g: (0, 0))
    wide = pl.BlockSpec((group, rows), lambda g: (g + low, 0))
    narrow = pl.BlockSpec((HEAD_SIZE, rows), lambda g: (g + low, 0))
    lse = pl.BlockSpec((1, 8, rows), lambda g: (g + low, 0, 0))
    return whole, table, wide, narrow, lse


def attention_forward(onehot, penalty, q, k, v):
    rows = q.shape[1]
    whole, table, wide, narrow, lse = attention_specs(rows)
    return pl.pallas_call(
        attention_forward_kernel,
        grid=(KEY_VALUE_HEADS,),
        in_specs=[whole, whole, wide, narrow, narrow],
        out_specs=[wide, lse],
        out_shape=[
            jax.ShapeDtypeStruct(q.shape, jnp.bfloat16),
            jax.ShapeDtypeStruct((KEY_VALUE_HEADS, 8, rows), jnp.float32),
        ],
        scratch_shapes=[pltpu.VMEM((rows, 2 * HEAD_SIZE), jnp.bfloat16)],
        compiler_params=pltpu.CompilerParams(vmem_limit_bytes=32 << 20),
        cost_estimate=pl.CostEstimate(
            flops=8 * 1153 * 10**6 * 2, transcendentals=0, bytes_accessed=8 << 20
        ),
        name="attention_forward",
    )(onehot, penalty, q, k, v)


def attention_backward(onehot, penalty, cos, sin, q, k, v, o, do, lse_rows, low, count):
    rows = q.shape[1]
    block = min(QUERY_BLOCK, rows)
    heads = QUERY_HEADS // KEY_VALUE_HEADS
    whole, table, wide, narrow, lse = attention_specs(rows, low)
    _, _, wide_out, narrow_out, _ = attention_specs(rows)
    return pl.pallas_call(
        attention_backward_kernel,
        grid=(count,),
        in_specs=[whole, whole, table, table, wide, narrow, narrow, wide, wide, lse],
        out_specs=[wide_out, narrow_out, narrow_out],
        out_shape=[
            jax.ShapeDtypeStruct((count * size, rows), jnp.bfloat16)
            for size in (heads * HEAD_SIZE, HEAD_SIZE, HEAD_SIZE)
        ],
        scratch_shapes=[
            pltpu.VMEM((rows, 2 * HEAD_SIZE), jnp.bfloat16),
            pltpu.VMEM((rows, 2 * HEAD_SIZE), jnp.bfloat16),
            pltpu.VMEM((rows // block, 2 * heads * block, 2 * HEAD_SIZE), jnp.bfloat16),
            pltpu.VMEM((rows, 2 * heads * block), jnp.bfloat16),
            pltpu.VMEM((rows, 2 * HEAD_SIZE), jnp.float32),
        ],
        compiler_params=pltpu.CompilerParams(vmem_limit_bytes=40 << 20),
        cost_estimate=pl.CostEstimate(
            flops=count * 6 * 1153 * 10**6, transcendentals=0, bytes_accessed=count * 5 << 19
        ),
        name="attention_backward",
    )(onehot, penalty, cos, sin, q, k, v, o, do, lse_rows)


def product_nt(left, right):
    return lax.dot_general(
        left, right, (((1,), (1,)), ((), ())), preferred_element_type=jnp.float32
    )


def contract(left, right, left_dim, right_dim):
    return lax.dot_general(
        left, right, (((left_dim,), (right_dim,)), ((), ())), preferred_element_type=jnp.float32
    )


def assemble_kernel(cuts, place_ref, *refs):
    units, outs, sems = refs[:8], refs[8:-1], refs[-1]
    copies = []
    for unit in range(8):
        y = place_ref[0] ^ (unit >> 2)
        d = (place_ref[1] ^ ((unit >> 1) & 1)) * 2 + (place_ref[2] ^ (unit & 1))
        for at, (low, high) in enumerate(cuts):
            copies.append(
                pltpu.make_async_copy(
                    units[unit].at[:, low:high], outs[at].at[d, :, y], sems.at[unit, at]
                )
            )
    for copy in copies:
        copy.start()
    for copy in copies:
        copy.wait()


def assemble_unaligned(place, units, rows):
    whole = jnp.stack(units).reshape((2, 2, 2) + units[0].shape)
    for axis in range(3):
        whole = jnp.where(place[axis] == 0, whole, jnp.flip(whole, axis))
    whole = whole.transpose(1, 2, 3, 0, 4, 5)
    cuts = [sum(rows[:i]) for i in range(len(rows) + 1)]
    parts = [whole[:, :, :, :, low:high] for low, high in zip(cuts, cuts[1:])]
    return [part.reshape(4, -1, part.shape[-1]) for part in parts]


def assemble(place, units, rows):
    nz, total, width = units[0].shape
    if any(r % 8 for r in rows) or any(r % 16 for r in rows[:-1]):
        return assemble_unaligned(place, units, rows)
    cuts = [(sum(rows[:i]), sum(rows[: i + 1])) for i in range(len(rows))]
    outs = pl.pallas_call(
        functools.partial(assemble_kernel, cuts),
        grid_spec=pltpu.PrefetchScalarGridSpec(
            num_scalar_prefetch=1,
            grid=(1,),
            in_specs=[pl.BlockSpec(memory_space=pl.ANY)] * 8,
            out_specs=[pl.BlockSpec(memory_space=pl.ANY)] * len(cuts),
            scratch_shapes=[pltpu.SemaphoreType.DMA((8, len(cuts)))],
        ),
        out_shape=[jax.ShapeDtypeStruct((4, nz, 2, r, width), jnp.bfloat16) for r in rows],
        compiler_params=pltpu.CompilerParams(vmem_limit_bytes=4 << 20),
        cost_estimate=pl.CostEstimate(
            flops=0, transcendentals=0, bytes_accessed=2 * 8 * nz * total * width * 2
        ),
        name="assemble",
    )(place, *units)
    return [out.reshape(4, nz * 2 * r, width) for out, r in zip(outs, rows)]


def feed_forward_kernel(
    place_ref, n2_ref, gy_ref, down_ref, *refs
):
    units = refs[:-12]
    (mixed_ref, dn2_ref, gu_send_ref, gu_keep_ref, od_send_ref, od_keep_ref) = refs[-12:-6]
    pieces, weights, n2_across, grads, hidden, sems = refs[-6:]
    step = pl.program_id(0)
    rows, width = n2_ref.shape
    nz, unit_rows, double = units[0].shape
    ff = double // 2
    block = min(ROW_BLOCK, rows)

    def copies(at):
        xr, cr = 1 - at % 2, 1 - at // 2
        made = []
        if len(units) == 1:
            whole = units[0].at[(place_ref[1] ^ xr) * 2 + (place_ref[2] ^ cr)]
            return [pltpu.make_async_copy(whole, pieces.at[at, 0], sems.at[at, 0])]
        for yr in range(2):
            y = place_ref[0] ^ yr
            for z in range(nz):
                made.append(
                    pltpu.make_async_copy(
                        units[yr * 4 + xr * 2 + cr].at[z],
                        pieces.at[at, 2 * z + y],
                        sems.at[at, yr * nz + z],
                    )
                )
        return made

    @pl.when(step == 0)
    def _():
        for at in range(4):
            for copy in copies(at):
                copy.start()
        n2_across[...] = n2_ref[...].T
        mixed_ref[...] = jnp.zeros_like(mixed_ref)
        dn2_ref[...] = jnp.zeros_like(dn2_ref)

    for at in range(4):

        @pl.when(step == at)
        def _():
            for copy in copies(at):
                copy.wait()

    for f in range(pieces.shape[1]):
        weights[f * pieces.shape[2] : (f + 1) * pieces.shape[2]] = pieces[step, f]

    def chunk(i, carry):
        part = pl.ds(pl.multiple_of(i * block, block), block)
        n2 = n2_ref[part]
        gate = product(n2, weights[:, :ff])
        up = product(n2, weights[:, ff:])
        sigma = jax.nn.sigmoid(gate)
        silu = gate * sigma
        hid = (silu * up).astype(jnp.bfloat16)
        hidden[part] = hid
        dhid = product_nt(gy_ref[0, part], down_ref[0])
        for d in range(1, 4):
            dhid = dhid + product_nt(gy_ref[d, part], down_ref[d])
        grads[part, :ff] = (dhid * up * (sigma * (1.0 + gate * (1.0 - sigma)))).astype(
            jnp.bfloat16
        )
        grads[part, ff:] = (dhid * silu).astype(jnp.bfloat16)
        for d in range(4):
            mixed_ref[d, part] = mixed_ref[d, part] + product(hid, down_ref[d])
        dn2_ref[part] = dn2_ref[part] + product_nt(grads[part], weights[...])
        return carry

    lax.fori_loop(0, rows // block, chunk, 0)

    def weight_grads(out_ref):
        for low in range(0, double, 256):
            out_ref[0, :, low : low + 256] = product(
                n2_across[...], grads[:, low : low + 256]
            ).astype(jnp.bfloat16)

    @pl.when(step < 2)
    def _():
        weight_grads(gu_send_ref)

    @pl.when(step >= 2)
    def _():
        weight_grads(gu_keep_ref)

    hidden_across = hidden[...].T
    own = od_send_ref.shape[1]
    depth = ff // own
    for cr, out_ref in ((1, od_send_ref), (0, od_keep_ref)):
        for k in range(2):
            d = (place_ref[1] ^ (1 - k)) * 2 + (place_ref[2] ^ cr)
            value = product(hidden_across, gy_ref[d]).astype(jnp.bfloat16)
            for f in range(own):
                out_ref[k, f, :depth] = value[f * depth : (f + 1) * depth]


def feed_forward(place, n2, gy, down, units, od_rows):
    rows, width = n2.shape
    fsdp, depth = 2 * units[0].shape[0], units[0].shape[1]
    if depth % 8:
        units = assemble(place, units, [depth])
        depth = width
    double = units[0].shape[2]
    ff = double // 2
    d_cols = gy.shape[2]
    own = fsdp // 4

    def hidden_block(s, place_ref):
        return (place_ref[1] ^ (1 - s % 2)) * 2 + (place_ref[2] ^ (1 - s // 2))

    once = pl.Buffered(1)
    flops = 2 * rows * width * 4 * ff * 9
    return pl.pallas_call(
        feed_forward_kernel,
        grid_spec=pltpu.PrefetchScalarGridSpec(
            num_scalar_prefetch=1,
            grid=(4,),
            in_specs=[
                pl.BlockSpec((rows, width), lambda s, p: (0, 0), pipeline_mode=once),
                pl.BlockSpec((4, rows, d_cols), lambda s, p: (0, 0, 0), pipeline_mode=once),
                pl.BlockSpec((4, ff, d_cols), lambda s, p: (0, hidden_block(s, p), 0)),
            ]
            + [pl.BlockSpec(memory_space=pl.ANY)] * len(units),
            out_specs=[
                pl.BlockSpec((4, rows, d_cols), lambda s, p: (0, 0, 0), pipeline_mode=once),
                pl.BlockSpec((rows, width), lambda s, p: (0, 0), pipeline_mode=once),
                pl.BlockSpec((1, width, double), lambda s, p: (jnp.minimum(s, 1), 0, 0)),
                pl.BlockSpec((1, width, double), lambda s, p: (jnp.maximum(s - 2, 0), 0, 0)),
                pl.BlockSpec((2, own, od_rows, d_cols), lambda s, p: (0, hidden_block(s, p), 0, 0)),
                pl.BlockSpec((2, own, od_rows, d_cols), lambda s, p: (0, hidden_block(s, p), 0, 0)),
            ],
            scratch_shapes=[
                pltpu.VMEM((4, width // depth, depth, double), jnp.bfloat16),
                pltpu.VMEM((width, double), jnp.bfloat16),
                pltpu.VMEM((width, rows), jnp.bfloat16),
                pltpu.VMEM((rows, double), jnp.bfloat16),
                pltpu.VMEM((rows, ff), jnp.bfloat16),
                pltpu.SemaphoreType.DMA((4, fsdp)),
            ],
        ),
        out_shape=[
            jax.ShapeDtypeStruct((4, rows, d_cols), jnp.float32),
            jax.ShapeDtypeStruct((rows, width), jnp.float32),
            jax.ShapeDtypeStruct((2, width, double), jnp.bfloat16),
            jax.ShapeDtypeStruct((2, width, double), jnp.bfloat16),
            jax.ShapeDtypeStruct((2, fsdp, od_rows, d_cols), jnp.bfloat16),
            jax.ShapeDtypeStruct((2, fsdp, od_rows, d_cols), jnp.bfloat16),
        ],
        compiler_params=pltpu.CompilerParams(vmem_limit_bytes=60 << 20),
        cost_estimate=pl.CostEstimate(flops=flops, transcendentals=0, bytes_accessed=48 << 20),
        name="feed_forward",
    )(place, n2, gy, down, *units)


def after(value, *others):
    return lax.optimization_barrier((value, *others))[0]


def swap(value, axes):
    count = 2 ** len(axes)
    return lax.ppermute(value, axes, [(i, count - 1 - i) for i in range(count)])


def z_partner(value, mask, nz):
    return lax.ppermute(value, "z", [(i, i ^ mask) for i in range(nz)])


def gather_z(shard, nz):
    if nz != 4:
        return lax.all_gather(shard, "z", axis=0, tiled=False)
    me = lax.axis_index("z")
    unit = jnp.zeros((nz,) + shard.shape, shard.dtype)
    for mask in range(nz):
        piece = z_partner(shard, mask, nz) if mask else shard
        unit = lax.dynamic_update_slice(unit, piece[None], (me ^ mask,) + (0,) * shard.ndim)
    return unit


def scatter_z(unit, nz):
    if nz != 4:
        return lax.psum_scatter(unit, "z", scatter_dimension=0, tiled=False).astype(jnp.float32)
    me = lax.axis_index("z")

    def part(mask):
        return lax.dynamic_index_in_dim(unit, me ^ mask, 0, keepdims=False)

    total = part(0).astype(jnp.float32)
    for mask in range(1, nz):
        total = total + z_partner(part(mask), mask, nz).astype(jnp.float32)
    return total


def units_of(own, along_y, along_x, along_both):
    four = (own, along_x, along_y, along_both)
    across = [swap(unit, ("c",)) for unit in four]
    order = []
    for yr in range(2):
        for xr in range(2):
            order += [four[yr * 2 + xr], across[yr * 2 + xr]]
    return order


def norm_back(values, scale_rows, gain_wide, upstream):
    weighted = gain_wide[None, :] * upstream
    return scale_rows * weighted - values * scale_rows**3 * jnp.mean(
        weighted * values, axis=1, keepdims=True
    )


def norm_scale(values):
    return lax.rsqrt(jnp.mean(values * values, axis=1, keepdims=True) + epsilon)


def shards(
    tokens,
    seq_lengths,
    norm1_gain,
    q_weight,
    k_weight,
    v_weight,
    o_weight,
    norm2_gain,
    gate_weight,
    up_weight,
    down_weight,
    cotangent,
):
    f32, bf16 = jnp.float32, jnp.bfloat16
    rows, width = tokens.shape
    nz = lax.axis_size("z")
    me_z, me_y, me_x, me_c = (lax.axis_index(a) for a in ("z", "y", "x", "c"))
    place = jnp.stack([me_y, me_x, me_c]).astype(jnp.int32)
    r_in, q_cols = q_weight.shape
    k_cols = k_weight.shape[1]
    qkv = q_cols + 2 * k_cols
    lanes = -(-(qkv + 2) // 128) * 128
    down_rows = down_weight.shape[0]
    o_rows = o_weight.shape[0]
    ff = gate_weight.shape[1]

    pack_a = jnp.concatenate(
        [
            q_weight,
            k_weight,
            v_weight,
            norm1_gain[:, None],
            norm2_gain[:, None],
            jnp.zeros((r_in, lanes - qkv - 2), bf16),
        ],
        axis=1,
    )
    filler = -(down_rows + o_rows) % 16
    pack_od = jnp.pad(jnp.concatenate([down_weight, o_weight], axis=0), ((0, filler), (0, 0)))
    pack_gu = jnp.concatenate([gate_weight, up_weight], axis=1)
    unit_a = gather_z(pack_a, nz)
    units_a = units_of(
        unit_a, swap(unit_a, ("y",)), swap(unit_a, ("x",)), swap(unit_a, ("y", "x"))
    )
    [weights_a] = assemble(place, units_a, [r_in])
    unit_od = gather_z(after(pack_od, unit_a), nz)
    unit_gu = gather_z(after(pack_gu, unit_a), nz)
    od_y, od_x = swap(unit_od, ("y",)), swap(unit_od, ("x",))
    gu_y, gu_x = swap(unit_gu, ("y",)), swap(unit_gu, ("x",))
    gain_one = weights_a[0, :, qkv].astype(f32)
    gain_two = weights_a[0, :, qkv + 1].astype(f32)

    lengths = seq_lengths[0]
    slots = jnp.arange(lengths.shape[0])
    ends = jnp.sum(jnp.where(slots[None, :] <= slots[:, None], lengths[None, :], 0), axis=1)
    places = jnp.arange(rows, dtype=jnp.int32)
    passed = (places[None, :] >= ends[:, None]).astype(jnp.int32)
    segment = jnp.sum(passed, axis=0)
    position = places - jnp.sum(passed * lengths[:, None], axis=0)
    live = (places < ends[-1]).astype(f32)
    same = jnp.arange(SEGMENT_ROWS)[:, None] == segment[None, :]
    onehot = same.astype(bf16)
    penalty = jnp.where(same, 0.0, masked_fill).astype(bf16)
    half = HEAD_SIZE // 2
    inverse = jnp.exp(
        -math.log(rope_base) * (jnp.arange(half, dtype=f32) * (2.0 / HEAD_SIZE))
    )
    angle = inverse[:, None] * position.astype(f32)[None, :]
    cos, sin = jnp.cos(angle), jnp.sin(angle)

    x = tokens.astype(f32)
    scale_one = norm_scale(x)
    n1 = (x * scale_one * gain_one[None, :]).astype(bf16)
    proj = lax.dot_general(
        weights_a, n1, (((1,), (1,)), ((), ())), preferred_element_type=f32
    )
    q_across = proj[:, :q_cols].reshape(QUERY_HEADS, 2, half, rows)
    k_across = proj[:, q_cols : q_cols + k_cols].reshape(KEY_VALUE_HEADS, 2, half, rows)
    v_across = proj[:, q_cols + k_cols : qkv].reshape(-1, rows).astype(bf16)

    def rope(u):
        u1, u2 = u[:, 0], u[:, 1]
        return (
            jnp.stack([u1 * cos - u2 * sin, u2 * cos + u1 * sin], axis=1)
            .astype(bf16)
            .reshape(-1, rows)
        )

    qr = rope(q_across) * jnp.asarray(1.0 / math.sqrt(HEAD_SIZE), bf16)
    kr = rope(k_across)
    qr = after(qr, unit_od, unit_gu)
    att, lse = attention_forward(onehot, penalty, qr, kr, v_across)
    od_y, od_x, gu_y, gu_x = (after(a, att) for a in (od_y, od_x, gu_y, gu_x))
    units_od = units_of(unit_od, od_y, od_x, swap(od_y, ("x",)))
    units_gu = units_of(unit_gu, gu_y, gu_x, swap(gu_x, ("y",)))
    down_all, o_all = assemble(place, units_od, [down_rows, o_rows + filler])
    o_all = o_all.reshape(4, 2 * nz, o_rows + filler, -1)[:, :, :o_rows].reshape(4, width, -1)
    o_full = jnp.concatenate([o_all[d] for d in range(4)], axis=1)
    hmid = x + contract(att, o_full, 0, 0)

    scale_two = norm_scale(hmid)
    n2 = (hmid * scale_two * gain_two[None, :]).astype(bf16)
    gy = live[:, None] * cotangent.astype(f32)
    d_cols = width // 4
    gy_low = gy.astype(bf16)
    gy_parts = jnp.stack([gy_low[:, d * d_cols : (d + 1) * d_cols] for d in range(4)])
    mixed_parts, dn2, gu_send, gu_keep, od_send, od_keep = feed_forward(
        place, n2, gy_parts, down_all, units_gu, down_rows + o_rows + filler
    )
    mixed = (
        live[:, None] * (hmid + jnp.concatenate([mixed_parts[d] for d in range(4)], axis=1))
    ).astype(bf16)
    grad_gain_two = jnp.sum(dn2 * hmid * scale_two, axis=0)
    dh = gy + norm_back(hmid, scale_two, gain_two, dn2)
    da = dh.astype(bf16)

    def quarter(halves, k, y):
        return lax.dynamic_index_in_dim(halves[k], y, 1, keepdims=False)

    gu_shape = (2, nz, 2, r_in, 2 * ff)
    gu_keep = gu_keep.reshape(gu_shape)
    gu_got = swap(gu_send, ("c",)).reshape(gu_shape)

    def both_gu(k, y):
        return quarter(gu_keep, k, y) + quarter(gu_got, k, y)

    gu_first = both_gu(0, 1 - me_y)
    gu_x = both_gu(0, me_y) + swap(gu_first, ("y",))
    gu_unit = both_gu(1, me_y) + swap(both_gu(1, 1 - me_y), ("y",)) + swap(gu_x, ("x",))
    sum_gu = scatter_z(gu_unit, nz)

    da_parts = jnp.stack([da[:, d * d_cols : (d + 1) * d_cols] for d in range(4)])
    grad_o = lax.dot_general(
        da_parts, att, (((1,), (1,)), ((), ())), preferred_element_type=f32
    )
    grad_o = grad_o.transpose(0, 2, 1).astype(bf16).reshape(2, 2, 2 * nz, o_rows, d_cols)
    datt = contract(o_full, da, 1, 1).astype(bf16)

    def with_o(parts, c):
        own = lax.dynamic_index_in_dim(grad_o, c, 1, keepdims=False)
        own = jnp.stack(
            [
                lax.dynamic_index_in_dim(own, 1 - me_x, 0, keepdims=False),
                lax.dynamic_index_in_dim(own, me_x, 0, keepdims=False),
            ]
        )
        return lax.dynamic_update_slice(parts, own, (0, 0, down_rows, 0))

    od_shape = (2, nz, 2, down_rows + o_rows + filler, d_cols)
    od_got = swap(with_o(od_send, 1 - me_c), ("c",)).reshape(od_shape)
    od_keep = with_o(od_keep, me_c).reshape(od_shape)

    def both_od(k, y):
        return quarter(od_keep, k, y) + quarter(od_got, k, y)

    od_first = both_od(0, 1 - me_y)
    od_y = both_od(1, 1 - me_y) + swap(od_first, ("x",))
    od_unit = both_od(1, me_y) + swap(both_od(0, me_y), ("x",)) + swap(od_y, ("y",))
    sum_od = scatter_z(od_unit, nz)

    back = functools.partial(attention_backward, onehot, penalty, cos, sin, qr, kr, v_across, att)
    first = back(after(datt, gu_first), lse, 0, 2)
    second = back(after(datt, od_first, first[0]), lse, 2, 3)
    dq, dk, dv = (jnp.concatenate(pair) for pair in zip(first, second))
    dproj = jnp.concatenate(
        [
            dq.reshape(4, q_cols, rows),
            dk.reshape(4, k_cols, rows),
            dv.reshape(4, k_cols, rows),
            jnp.zeros((4, lanes - qkv, rows), bf16),
        ],
        axis=1,
    )
    grad_a = lax.dot_general(dproj, n1, (((2,), (0,)), ((), ())), preferred_element_type=f32)
    grad_a = grad_a.transpose(0, 2, 1).astype(bf16).reshape(2, 2, nz, 2, r_in, lanes)
    a_send = lax.dynamic_index_in_dim(grad_a, 1 - me_c, 1, keepdims=False)
    a_keep = lax.dynamic_index_in_dim(grad_a, me_c, 1, keepdims=False)
    dn1 = lax.dot_general(
        dproj, weights_a, (((0, 1), (0, 2)), ((), ())), preferred_element_type=f32
    )
    gains = jnp.stack([jnp.sum(dn1 * x * scale_one, axis=0), grad_gain_two], axis=1)
    gains = (gains + swap(gains.astype(bf16), ("c",)).astype(f32)).astype(bf16)
    gains = jnp.pad(gains, ((0, 0), (qkv, lanes - qkv - 2)))
    gains = gains.reshape(1, nz, 2, r_in, lanes)
    a_sum = a_keep + swap(a_send, ("c",)) + gains

    def part_a(x, y):
        return lax.dynamic_index_in_dim(
            lax.dynamic_index_in_dim(a_sum, x, 0, keepdims=False), y, 1, keepdims=False
        )

    a_unit = (
        part_a(me_x, me_y)
        + swap(part_a(1 - me_x, me_y), ("x",))
        + swap(part_a(me_x, 1 - me_y), ("y",))
        + swap(part_a(1 - me_x, 1 - me_y), ("y", "x"))
    )
    sum_a = scatter_z(a_unit, nz)
    grad_tokens = dh + norm_back(x, scale_one, gain_one, dn1)
    return (
        mixed,
        grad_tokens,
        sum_a[:, qkv],
        sum_a[:, :q_cols],
        sum_a[:, q_cols : q_cols + k_cols],
        sum_a[:, q_cols + k_cols : qkv],
        sum_od[down_rows : down_rows + o_rows],
        sum_a[:, qkv + 1],
        sum_gu[:, :ff],
        sum_gu[:, ff:],
        sum_od[:down_rows],
    )


def solution(mesh):
    fsdp, dp = mesh.devices.shape
    assert dp == 4 and fsdp % 2 == 0
    split = Mesh(mesh.devices.reshape(fsdp // 2, 2, 2, 2), ("z", "y", "x", "c"))
    rows, grid, gain = P(("z", "y", "x", "c"), None), P(("z", "y"), ("x", "c")), P(("z", "y"))
    return jax.shard_map(
        shards,
        mesh=split,
        in_specs=(rows, rows, gain, grid, grid, grid, grid, gain, grid, grid, grid, rows),
        out_specs=(rows, rows, gain, grid, grid, grid, grid, gain, grid, grid, grid),
        check_vma=False,
    )
```

time: 852 us -> 486 us (0.57)
  the two profiles are of different devices: /device:TPU:0 before, /device:TPU:14 now
where the time goes in v2:
time: 486 us; the launch traced here: 477 us
  waiting for transfers between devices  146 us (30%)
  Pallas kernels  129 us (27%)
  local copies, waits for them, and re-layouts  86.2 us (18%)
  starting transfers between devices  43.1 us (9%)
  other arithmetic  41.9 us (9%)
  matrix products  29.2 us (6%)
    ppermute x18, waiting for transfers between devices, z_partner(): return lax.ppermute(value, 'z', [(i, i ^ mask) for i in range(nz)])  91.3 us
    pallas_call x1, Pallas kernels, feed_forward(): pl.pallas_call(feed_forward_kernel, grid_spec=pltpu.PrefetchScalarGridSpe...  68.2 us
    ppermute x34, waiting for transfers between devices, swap(): return lax.ppermute(value, axes, [(i, count - 1 - i) for i in range(count)])  54.5 us
    unnamed x141, local copies, waits for them, and re-layouts  47.6 us
    pallas_call x2, Pallas kernels, attention_backward(): pl.pallas_call(attention_backward_kernel, grid=(count,), in_specs=[whole,...  31.3 us
    pallas_call x1, Pallas kernels, attention_forward(): pl.pallas_call(attention_forward_kernel, grid=(KEY_VALUE_HEADS,), in_spec...  24.3 us
    ppermute x18, starting transfers between devices, z_partner(): return lax.ppermute(value, 'z', [(i, i ^ mask) for i in range(nz)])  21.6 us
    ppermute x34, starting transfers between devices, swap(): return lax.ppermute(value, axes, [(i, count - 1 - i) for i in range(count)])  21.4 us
  transfers between devices with their start and end apart: 52, of which 20 were waited for; matrix products, arithmetic and copies ran while one was open for 22% of the time, Pallas kernels for 13%

profile of v2, /device:TPU:14, one launch (start us, length us, event | category | flops | bytes accessed | tf_op | source)
XLA Modules:
  0.0 476.9 jit_solution(16589569269775349864)
XLA Ops:
  5.4 2.6 collective-permute-start.1
  10.0 2.8 copy.180
  16.8 2.3 collective-permute-done.2
  20.3 2.4 collective-permute-start.8
  27.6 7.0 %collective-permute-done.10 = bf16[448,240]{1,0:T(8,128)(2,1)S(1)} collective-permute-done((bf16[448,240]{1,0:T(8,128)(2,1)S(1)}, bf16[448,240]{1,0:T(8,128)(2,1)S(1)}, u32[]{:S(2)}, u32[]{:S(2)}) %collective-permute-start.10) | collective-permute-done | bytes 215072 | tf_op jit(solution)/shard_map/ppermute | solution.py:449
  36.8 8.5 %collective-permute-done.11 = bf16[448,240]{1,0:T(8,128)(2,1)S(1)} collective-permute-done((bf16[448,240]{1,0:T(8,128)(2,1)S(1)}, bf16[448,240]{1,0:T(8,128)(2,1)S(1)}, u32[]{:S(2)}, u32[]{:S(2)}) %collective-permute-start.11) | collective-permute-done | bytes 215072 | tf_op jit(solution)/shard_map/ppermute | solution.py:449
  45.7 8.6 %collective-permute-done.12 = bf16[448,240]{1,0:T(8,128)(2,1)S(1)} collective-permute-done((bf16[448,240]{1,0:T(8,128)(2,1)S(1)}, bf16[448,240]{1,0:T(8,128)(2,1)S(1)}, u32[]{:S(2)}, u32[]{:S(2)}) %collective-permute-start.12) | collective-permute-done | bytes 215072 | tf_op jit(solution)/shard_map/ppermute | solution.py:449
  54.3 2.4 collective-permute-start.14
  57.4 13.4 %collective-permute-done.14 = bf16[120,1280]{1,0:T(8,128)(2,1)S(1)} collective-permute-done((bf16[120,1280]{1,0:T(8,128)(2,1)}, bf16[120,1280]{1,0:T(8,128)(2,1)S(1)}, u32[]{:S(2)}, u32[]{:S(2)}) %collective-permute-start.14) | collective-permute-done | bytes 307232 | tf_op jit(solution)/shard_map/ppermute | solution.py:449
  72.5 14.0 %collective-permute-done.15 = bf16[120,1280]{1,0:T(8,128)(2,1)S(1)} collective-permute-done((bf16[120,1280]{1,0:T(8,128)(2,1)}, bf16[120,1280]{1,0:T(8,128)(2,1)S(1)}, u32[]{:S(2)}, u32[]{:S(2)}) %collective-permute-start.15) | collective-permute-done | bytes 307232 | tf_op jit(solution)/shard_map/ppermute | solution.py:449
  96.4 7.6 %fusion.35 = f32[4,512,1024]{2,1,0:T(8,128)S(1)} fusion(bf16[4,960,512]{2,1,0:T(8,128)(2,1)} %bitcast.258, bf16[1024,960]{1,0:T(8,128)(2,1)} %copy-done.15, f32[960]{0:T(1024)S(1)} %bitcast.310, f32[1024]{0:T(1024)S(1)} %get-tuple-element.182), kind=kOutput, calls=%fused_computation.61 | convolution fusion | flops 4030464000 | bytes 14294784 | tf_op jit(solution)/shard_map/dot_general | solution.py:572
  105.9 24.3 %attention_forward.1 = (bf16[960,1024]{1,0:T(8,128)(2,1)S(1)}, f32[5,8,1024]{2,1,0:T(8,128)S(1)}) custom-call(bf16[16,1024]{1,0:T(8,128)(2,1)S(1)} %fusion.55.onehot_ref, bf16[16,1024]{1,0:T(8,128)(2,1)S(1)} %select_convert_fusion.penalty_ref, bf16[960,1024]{1,0:T(8,128)(2,1)S(1)} %bitcast.260, bf16[320,1024]{1,0:T(8,128)(2,1)S(1)} %bitcast.267, ...), custom_call_target="tpu_custom_call" | custom-call | flops 18447998976 | bytes 8388608 | tf_op jit(solution)/shard_map/attention_forward/pallas_call | solution.py:172
  132.0 5.4 %collective-permute-done.24.refs_2_ = bf16[4,120,1280]{2,1,0:T(8,128)(2,1)} collective-permute-done((bf16[4,120,1280]{2,1,0:T(8,128)(2,1)}, bf16[4,120,1280]{2,1,0:T(8,128)(2,1)}, u32[]{:S(2)}, u32[]{:S(2)}) %collective-permute-start.24) | collective-permute-done | bytes 1228832 | tf_op jit(solution)/shard_map/ppermute | solution.py:445
  140.1 14.5 %collective-permute-done.21.refs_6_ = bf16[4,448,240]{2,1,0:T(8,128)(2,1)} collective-permute-done((bf16[4,448,240]{2,1,0:T(8,128)(2,1)}, bf16[4,448,240]{2,1,0:T(8,128)(2,1)}, u32[]{:S(2)}, u32[]{:S(2)}) %collective-permute-start.21) | collective-permute-done | bytes 860192 | tf_op jit(solution)/shard_map/ppermute | solution.py:445
  155.3 3.9 copy.189
  166.3 3.6 assemble.3
  169.9 2.4 copy-done.7
  174.5 2.8 multiply_reduce_fusion.2
  184.2 68.2 %feed_forward.1 = (f32[4,1024,240]{2,1,0:T(8,128)}, f32[1024,960]{1,0:T(8,128)}, bf16[2,960,1280]{2,1,0:T(8,128)(2,1)}, bf16[2,960,1280]{2,1,0:T(8,128)(2,1)}, b...) custom-call(s32[3]{0:T(128)} %copy-done.6, bf16[1024,960]{1,0:T(8,128)(2,1)} %multiply_convert_fusion.n2_ref, ...), custom_call_target="tpu_custom_call" | custom-call | flops 45298483200 | bytes 50331648 | tf_op jit(solution)/shard_map/feed_forward/pallas_call | solution.py:397
  252.4 2.6 slice_bitcast_fusion.3
  258.7 4.9 %fusion.62 = (bf16[1024,960]{1,0:T(8,128)(2,1)S(1)}, f32[1024,960]{1,0:T(8,128)}, bf16[1024,960]{1,0:T(8,128)(2,1)}) fusion(f32[1024]{0:T(1024)S(1)} %broadcast_multiply_fusion.1, f32[1024,960]{1,0:T(8,128)S(1)} %copy-done.14, f32[1024]{0:T(1024)S(1)} %get-tuple-element.183, f32[1024,960]{1,0:T(8,128)S(1)} %copy-done.19, f32[960]{0:T(1024)S(1)} %bitcast.307, ...), kind=kLoop, calls=%fused_computation.169 | loop fusion | flops 14745600 | bytes 21647104 | tf_op jit(solution)/shard_map/convert_element_type | solution.py:613
  265.9 3.7 convert_bitcast_fusion
  269.6 3.9 copy.230
  277.9 3.7 fusion.65
  283.1 3.7 fusion.66
  289.5 3.5 convolution_convert_fusion.1.do_ref
  293.0 3.9 copy.217
  297.0 2.9 fusion.63
  300.8 11.0 %collective-permute-done.41 = bf16[4,448,240]{2,1,0:T(8,128)(2,1)} collective-permute-done((bf16[4,448,240]{2,1,0:T(8,128)(2,1)}, bf16[4,448,240]{2,1,0:T(8,128)(2,1)}, u32[]{:S(2)}, u32[]{:S(2)}) %collective-permute-start.41) | collective-permute-done | bytes 860192 | tf_op jit(solution)/shard_map/ppermute | solution.py:445
  311.7 2.3 fusion.38
  315.6 2.9 fusion.64
  322.6 12.5 %attention_backward.2 = (bf16[384,1024]{1,0:T(8,128)(2,1)S(1)}, bf16[128,1024]{1,0:T(8,128)(2,1)S(1)}, bf16[128,1024]{1,0:T(8,128)(2,1)S(1)}) custom-call(bf16[16,1024]{1,0:T(8,128)(2,1)S(1)} %fusion.55.onehot_ref, bf16[16,1024]{1,0:T(8,128)(2,1)S(1)} %select_convert_fusion.penalty_ref, f32[32,1024]{1,0:T(8,128)S(1)} %get-tuple-element.179.cos_ref, ...), custom_call_target="tpu_custom_call" | custom-call | flops 13836000256 | bytes 5242880 | tf_op jit(solution)/shard_map/attention_backward/pallas_call | solution.py:196
  335.1 18.8 %attention_backward.3 = (bf16[576,1024]{1,0:T(8,128)(2,1)S(1)}, bf16[192,1024]{1,0:T(8,128)(2,1)S(1)}, bf16[192,1024]{1,0:T(8,128)(2,1)S(1)}) custom-call(bf16[16,1024]{1,0:T(8,128)(2,1)S(1)} %fusion.55.onehot_ref, bf16[16,1024]{1,0:T(8,128)(2,1)S(1)} %select_convert_fusion.penalty_ref, f32[32,1024]{1,0:T(8,128)S(1)} %get-tuple-element.179.cos_ref, ...), custom_call_target="tpu_custom_call" | custom-call | flops 20753999872 | bytes 7864320 | tf_op jit(solution)/shard_map/attention_backward/pallas_call | solution.py:196
  355.7 4.6 convolution_convert_fusion
  361.7 2.8 copy-done.1
  364.5 7.1 %fusion.8 = (f32[960]{0:T(1024)S(1)}, f32[1024]{0:T(1024)S(1)}, f32[1024,960,1]{1,0,2:T(8,128)}) fusion(bf16[1024,960]{1,0:T(8,128)(2,1)S(1)} %copy-done.17, f32[1024]{0:T(1024)S(1)} %copy-done.60, f32[960]{0:T(1024)S(1)} %bitcast.312, bf16[4,960,512]{2,1,0:T(8,128)(2,1)S(1)} %bitcast.259, bf16[4,80,1024]{2,1,0:T(8,128)(2,1)S(1)} %bitcast.296, ...), kind=kOutput, calls=%fused_computation.14 | convolution fusion | flops 4050188288 | bytes 13124096 | tf_op jit(solution)/shard_map/dot_general | solution.py:676
  374.8 3.0 fusion.42
  381.4 2.6 fusion.28
  384.4 2.2 fusion.21
  390.5 5.2 %collective-permute-done.44 = bf16[448,240]{1,0:T(8,128)(2,1)S(1)} collective-permute-done((bf16[448,240]{1,0:T(8,128)(2,1)S(1)}, bf16[448,240]{1,0:T(8,128)(2,1)S(1)}, u32[]{:S(2)}, u32[]{:S(2)}) %collective-permute-start.44) | collective-permute-done | bytes 215072 | tf_op jit(solution)/shard_map/ppermute | solution.py:449
  397.3 4.3 collective-permute-done.45
  403.0 2.7 fusion.5
  405.7 5.4 %copy.218 = f32[1024,960]{0,1:T(8,128)} copy(f32[1024,960]{1,0:T(8,128)} %fusion.5) | data formatting | bytes 7864320
  412.6 12.2 %collective-permute-done.34 = bf16[4,120,512]{2,1,0:T(8,128)(2,1)} collective-permute-done((bf16[4,120,512]{2,1,0:T(8,128)(2,1)}, bf16[4,120,512]{2,1,0:T(8,128)(2,1)}, u32[]{:S(2)}, u32[]{:S(2)}) %collective-permute-start.34) | collective-permute-done | bytes 491552 | tf_op jit(solution)/shard_map/ppermute | solution.py:445
  424.8 9.9 %collective-permute-done.36 = bf16[4,120,512]{2,1,0:T(8,128)(2,1)} collective-permute-done((bf16[4,120,512]{2,1,0:T(8,128)(2,1)S(1)}, bf16[4,120,512]{2,1,0:T(8,128)(2,1)}, u32[]{:S(2)}, u32[]{:S(2)}) %collective-permute-start.36) | collective-permute-done | bytes 491552 | tf_op jit(solution)/shard_map/ppermute | solution.py:445
  445.6 5.2 %collective-permute-done.39 = bf16[120,512]{1,0:T(8,128)(2,1)S(1)} collective-permute-done((bf16[120,512]{1,0:T(8,128)(2,1)S(1)}, bf16[120,512]{1,0:T(8,128)(2,1)S(1)}, u32[]{:S(2)}, u32[]{:S(2)}) %collective-permute-start.39) | collective-permute-done | bytes 122912 | tf_op jit(solution)/shard_map/ppermute | solution.py:449
  455.2 13.4 %collective-permute-done.50 = bf16[120,1280]{1,0:T(8,128)(2,1)S(1)} collective-permute-done((bf16[120,1280]{1,0:T(8,128)(2,1)S(1)}, bf16[120,1280]{1,0:T(8,128)(2,1)S(1)}, u32[]{:S(2)}, u32[]{:S(2)}) %collective-permute-start.50) | collective-permute-done | bytes 307232 | tf_op jit(solution)/shard_map/ppermute | solution.py:449
  468.6 6.8 %collective-permute-done.51 = bf16[120,1280]{1,0:T(8,128)(2,1)S(1)} collective-permute-done((bf16[120,1280]{1,0:T(8,128)(2,1)S(1)}, bf16[120,1280]{1,0:T(8,128)(2,1)S(1)}, u32[]{:S(2)}, u32[]{:S(2)}) %collective-permute-start.51) | collective-permute-done | bytes 307232 | tf_op jit(solution)/shard_map/ppermute | solution.py:449
  (301 shorter events, 110.9 us)
Async XLA Ops:
  4.9 10.8 %collective-permute-start = (bf16[120,512]{1,0:T(8,128)(2,1)S(1)}, bf16[120,512]{1,0:T(8,128)(2,1)S(1)}, u32[]{:S(2)}, u32[]{:S(2)}) collective-permute-start(bf16[120,512]{1,0:T(8,128)(2,1)S(1)} %concatenate.27), channel_id=1, source_target_pairs={{0,8},{8,0},{16,24},{24,16},{1,9},{9,1},{17,25},{25,17},{2,10},{10... | collective-permute-start | bytes 368648 | tf_op jit(solution)/shard_map/ppermute | solution.py:449
  5.4 11.4 %collective-permute-start.1 = (bf16[120,512]{1,0:T(8,128)(2,1)S(1)}, bf16[120,512]{1,0:T(8,128)(2,1)S(1)}, u32[]{:S(2)}, u32[]{:S(2)}) collective-permute-start(bf16[120,512]{1,0:T(8,128)(2,1)S(1)} %concatenate.27), channel_id=1, source_target_pairs={{0,16},{8,24},{16,0},{24,8},{1,17},{9,25},{17,1},{25,9},{2,18},{10... | collective-permute-start | bytes 368648 | tf_op jit(solution)/shard_map/ppermute | solution.py:449
  8.0 11.2 %collective-permute-start.2 = (bf16[120,512]{1,0:T(8,128)(2,1)S(1)}, bf16[120,512]{1,0:T(8,128)(2,1)S(1)}, u32[]{:S(2)}, u32[]{:S(2)}) collective-permute-start(bf16[120,512]{1,0:T(8,128)(2,1)S(1)} %concatenate.27), channel_id=1, source_target_pairs={{0,24},{8,16},{16,8},{24,0},{1,25},{9,17},{17,9},{25,1},{2,26},{10... | collective-permute-start | bytes 368648 | tf_op jit(solution)/shard_map/ppermute | solution.py:449
  19.1 52.0 %collective-permute-start.4 = (bf16[4,120,512]{2,1,0:T(8,128)(2,1)S(1)}, bf16[4,120,512]{2,1,0:T(8,128)(2,1)S(1)}, u32[]{:S(2)}, u32[]{:S(2)}) collective-permute-start(bf16[4,120,512]{2,1,0:T(8,128)(2,1)S(1)} %bitcast_dynamic-update-slice_fusion.8.refs_0_), channel_id=1, source_target_pairs={{0,2},{2,0},{1,3},{3,1},{4,6},{6,4},{5,7},{7,5},{8,10},{10,8},{9,1... | collective-permute-start | bytes 1474568 | tf_op jit(solution)/shard_map/ppermute | solution.py:445
  19.7 51.4 %collective-permute-start.6 = (bf16[4,120,512]{2,1,0:T(8,128)(2,1)S(1)}, bf16[4,120,512]{2,1,0:T(8,128)(2,1)S(1)}, u32[]{:S(2)}, u32[]{:S(2)}) collective-permute-start(bf16[4,120,512]{2,1,0:T(8,128)(2,1)S(1)} %bitcast_dynamic-update-slice_fusion.8.refs_0_), channel_id=1, source_target_pairs={{0,4},{4,0},{1,5},{5,1},{2,6},{6,2},{3,7},{7,3},{8,12},{12,8},{9,1... | collective-permute-start | bytes 1474568 | tf_op jit(solution)/shard_map/ppermute | solution.py:445
  20.3 51.4 %collective-permute-start.8 = (bf16[4,120,512]{2,1,0:T(8,128)(2,1)S(1)}, bf16[4,120,512]{2,1,0:T(8,128)(2,1)S(1)}, u32[]{:S(2)}, u32[]{:S(2)}) collective-permute-start(bf16[4,120,512]{2,1,0:T(8,128)(2,1)S(1)} %bitcast_dynamic-update-slice_fusion.8.refs_0_), channel_id=1, source_target_pairs={{0,6},{2,4},{4,2},{6,0},{1,7},{3,5},{5,3},{7,1},{8,14},{10,12},{12... | collective-permute-start | bytes 1474568 | tf_op jit(solution)/shard_map/ppermute | solution.py:445
  22.7 31.6 %collective-permute-start.13 = (bf16[120,1280]{1,0:T(8,128)(2,1)}, bf16[120,1280]{1,0:T(8,128)(2,1)S(1)}, u32[]{:S(2)}, u32[]{:S(2)}) collective-permute-start(bf16[120,1280]{1,0:T(8,128)(2,1)} %pad_maximum_fusion.8), channel_id=1, source_target_pairs={{0,8},{8,0},{16,24},{24,16},{1,9},{9,1},{17,25},{25,17},{2,10},{10... | collective-permute-start | bytes 921608 | tf_op jit(solution)/shard_map/ppermute | solution.py:449
  25.7 8.9 %collective-permute-start.10 = (bf16[448,240]{1,0:T(8,128)(2,1)S(1)}, bf16[448,240]{1,0:T(8,128)(2,1)S(1)}, u32[]{:S(2)}, u32[]{:S(2)}) collective-permute-start(bf16[448,240]{1,0:T(8,128)(2,1)S(1)} %fusion.54), channel_id=1, source_target_pairs={{0,8},{8,0},{16,24},{24,16},{1,9},{9,1},{17,25},{25,17},{2,10},{10... | collective-permute-start | bytes 645128 | tf_op jit(solution)/shard_map/ppermute | solution.py:449
  34.6 10.7 %collective-permute-start.11 = (bf16[448,240]{1,0:T(8,128)(2,1)S(1)}, bf16[448,240]{1,0:T(8,128)(2,1)S(1)}, u32[]{:S(2)}, u32[]{:S(2)}) collective-permute-start(bf16[448,240]{1,0:T(8,128)(2,1)S(1)} %fusion.54), channel_id=1, source_target_pairs={{0,16},{8,24},{16,0},{24,8},{1,17},{9,25},{17,1},{25,9},{2,18},{10... | collective-permute-start | bytes 645128 | tf_op jit(solution)/shard_map/ppermute | solution.py:449
  45.3 9.0 %collective-permute-start.12 = (bf16[448,240]{1,0:T(8,128)(2,1)S(1)}, bf16[448,240]{1,0:T(8,128)(2,1)S(1)}, u32[]{:S(2)}, u32[]{:S(2)}) collective-permute-start(bf16[448,240]{1,0:T(8,128)(2,1)S(1)} %fusion.54), channel_id=1, source_target_pairs={{0,24},{8,16},{16,8},{24,0},{1,25},{9,17},{17,9},{25,1},{2,26},{10... | collective-permute-start | bytes 645128 | tf_op jit(solution)/shard_map/ppermute | solution.py:449
  54.3 33.5 %collective-permute-start.3 = (bf16[4,120,512]{2,1,0:T(8,128)(2,1)S(1)}, bf16[4,120,512]{2,1,0:T(8,128)(2,1)S(1)}, u32[]{:S(2)}, u32[]{:S(2)}) collective-permute-start(bf16[4,120,512]{2,1,0:T(8,128)(2,1)S(1)} %bitcast_dynamic-update-slice_fusion.8.refs_0_), channel_id=1, source_target_pairs={{0,1},{1,0},{2,3},{3,2},{4,5},{5,4},{6,7},{7,6},{8,9},{9,8},{10,11... | collective-permute-start | bytes 1474568 | tf_op jit(solution)/shard_map/ppermute | solution.py:445
  54.3 16.5 %collective-permute-start.14 = (bf16[120,1280]{1,0:T(8,128)(2,1)}, bf16[120,1280]{1,0:T(8,128)(2,1)S(1)}, u32[]{:S(2)}, u32[]{:S(2)}) collective-permute-start(bf16[120,1280]{1,0:T(8,128)(2,1)} %pad_maximum_fusion.8), channel_id=1, source_target_pairs={{0,16},{8,24},{16,0},{24,8},{1,17},{9,25},{17,1},{25,9},{2,18},{10... | collective-permute-start | bytes 921608 | tf_op jit(solution)/shard_map/ppermute | solution.py:449
  70.8 15.7 %collective-permute-start.15 = (bf16[120,1280]{1,0:T(8,128)(2,1)}, bf16[120,1280]{1,0:T(8,128)(2,1)S(1)}, u32[]{:S(2)}, u32[]{:S(2)}) collective-permute-start(bf16[120,1280]{1,0:T(8,128)(2,1)} %pad_maximum_fusion.8), channel_id=1, source_target_pairs={{0,24},{8,16},{16,8},{24,0},{1,25},{9,17},{17,9},{25,1},{2,26},{10... | collective-permute-start | bytes 921608 | tf_op jit(solution)/shard_map/ppermute | solution.py:449
  71.1 17.1 %collective-permute-start.5 = (bf16[4,120,512]{2,1,0:T(8,128)(2,1)S(1)}, bf16[4,120,512]{2,1,0:T(8,128)(2,1)S(1)}, u32[]{:S(2)}, u32[]{:S(2)}) collective-permute-start(bf16[4,120,512]{2,1,0:T(8,128)(2,1)S(1)} %collective-permute-done.4.refs_2_), channel_id=1, source_target_pairs={{0,1},{1,0},{2,3},{3,2},{4,5},{5,4},{6,7},{7,6},{8,9},{9,8},{10,11... | collective-permute-start | bytes 1474568 | tf_op jit(solution)/shard_map/ppermute | solution.py:445
  71.2 18.6 %collective-permute-start.7 = (bf16[4,120,512]{2,1,0:T(8,128)(2,1)S(1)}, bf16[4,120,512]{2,1,0:T(8,128)(2,1)S(1)}, u32[]{:S(2)}, u32[]{:S(2)}) collective-permute-start(bf16[4,120,512]{2,1,0:T(8,128)(2,1)S(1)} %collective-permute-done.6.refs_4_), channel_id=1, source_target_pairs={{0,1},{1,0},{2,3},{3,2},{4,5},{5,4},{6,7},{7,6},{8,9},{9,8},{10,11... | collective-permute-start | bytes 1474568 | tf_op jit(solution)/shard_map/ppermute | solution.py:445
  71.7 19.6 %collective-permute-start.9 = (bf16[4,120,512]{2,1,0:T(8,128)(2,1)S(1)}, bf16[4,120,512]{2,1,0:T(8,128)(2,1)S(1)}, u32[]{:S(2)}, u32[]{:S(2)}) collective-permute-start(bf16[4,120,512]{2,1,0:T(8,128)(2,1)S(1)} %collective-permute-done.8.refs_6_), channel_id=1, source_target_pairs={{0,1},{1,0},{2,3},{3,2},{4,5},{5,4},{6,7},{7,6},{8,9},{9,8},{10,11... | collective-permute-start | bytes 1474568 | tf_op jit(solution)/shard_map/ppermute | solution.py:445
  86.5 45.0 %collective-permute-start.19 = (bf16[4,448,240]{2,1,0:T(8,128)(2,1)S(1)}, bf16[4,448,240]{2,1,0:T(8,128)(2,1)}, u32[]{:S(2)}, u32[]{:S(2)}) collective-permute-start(bf16[4,448,240]{2,1,0:T(8,128)(2,1)S(1)} %bitcast_dynamic-update-slice_fusion.4.refs_0_), channel_id=1, source_target_pairs={{0,4},{4,0},{1,5},{5,1},{2,6},{6,2},{3,7},{7,3},{8,12},{12,8},{9,1... | collective-permute-start | bytes 2580488 | tf_op jit(solution)/shard_map/ppermute | solution.py:445
  87.7 51.8 %collective-permute-start.17 = (bf16[4,448,240]{2,1,0:T(8,128)(2,1)S(1)}, bf16[4,448,240]{2,1,0:T(8,128)(2,1)}, u32[]{:S(2)}, u32[]{:S(2)}) collective-permute-start(bf16[4,448,240]{2,1,0:T(8,128)(2,1)S(1)} %bitcast_dynamic-update-slice_fusion.4.refs_0_), channel_id=1, source_target_pairs={{0,2},{2,0},{1,3},{3,1},{4,6},{6,4},{5,7},{7,5},{8,10},{10,8},{9,1... | collective-permute-start | bytes 2580488 | tf_op jit(solution)/shard_map/ppermute | solution.py:445
  88.3 49.2 %collective-permute-start.24 = (bf16[4,120,1280]{2,1,0:T(8,128)(2,1)}, bf16[4,120,1280]{2,1,0:T(8,128)(2,1)}, u32[]{:S(2)}, u32[]{:S(2)}) collective-permute-start(bf16[4,120,1280]{2,1,0:T(8,128)(2,1)} %bitcast_dynamic-update-slice_fusion.refs_0_), channel_id=1, source_target_pairs={{0,2},{2,0},{1,3},{3,1},{4,6},{6,4},{5,7},{7,5},{8,10},{10,8},{9,1... | collective-permute-start | bytes 3686408 | tf_op jit(solution)/shard_map/ppermute | solution.py:445
  89.8 50.3 %collective-permute-start.26 = (bf16[4,120,1280]{2,1,0:T(8,128)(2,1)}, bf16[4,120,1280]{2,1,0:T(8,128)(2,1)}, u32[]{:S(2)}, u32[]{:S(2)}) collective-permute-start(bf16[4,120,1280]{2,1,0:T(8,128)(2,1)} %bitcast_dynamic-update-slice_fusion.refs_0_), channel_id=1, source_target_pairs={{0,4},{4,0},{1,5},{5,1},{2,6},{6,2},{3,7},{7,3},{8,12},{12,8},{9,1... | collective-permute-start | bytes 3686408 | tf_op jit(solution)/shard_map/ppermute | solution.py:445
  131.5 23.2 %collective-permute-start.21 = (bf16[4,448,240]{2,1,0:T(8,128)(2,1)}, bf16[4,448,240]{2,1,0:T(8,128)(2,1)}, u32[]{:S(2)}, u32[]{:S(2)}) collective-permute-start(bf16[4,448,240]{2,1,0:T(8,128)(2,1)} %collective-permute-done.19.refs_4_), channel_id=1, source_target_pairs={{0,2},{2,0},{1,3},{3,1},{4,6},{6,4},{5,7},{7,5},{8,10},{10,8},{9,1... | collective-permute-start | bytes 2580488 | tf_op jit(solution)/shard_map/ppermute | solution.py:445
  137.5 28.8 %collective-permute-start.28 = (bf16[4,120,1280]{2,1,0:T(8,128)(2,1)}, bf16[4,120,1280]{2,1,0:T(8,128)(2,1)}, u32[]{:S(2)}, u32[]{:S(2)}) collective-permute-start(bf16[4,120,1280]{2,1,0:T(8,128)(2,1)} %collective-permute-done.24.refs_2_), channel_id=1, source_target_pairs={{0,4},{4,0},{1,5},{5,1},{2,6},{6,2},{3,7},{7,3},{8,12},{12,8},{9,1... | collective-permute-start | bytes 3686408 | tf_op jit(solution)/shard_map/ppermute | solution.py:445
  139.6 25.6 %collective-permute-start.16 = (bf16[4,448,240]{2,1,0:T(8,128)(2,1)S(1)}, bf16[4,448,240]{2,1,0:T(8,128)(2,1)}, u32[]{:S(2)}, u32[]{:S(2)}) collective-permute-start(bf16[4,448,240]{2,1,0:T(8,128)(2,1)S(1)} %bitcast_dynamic-update-slice_fusion.4.refs_0_), channel_id=1, source_target_pairs={{0,1},{1,0},{2,3},{3,2},{4,5},{5,4},{6,7},{7,6},{8,9},{9,8},{10,11... | collective-permute-start | bytes 2580488 | tf_op jit(solution)/shard_map/ppermute | solution.py:445
  139.6 26.1 %collective-permute-start.20 = (bf16[4,448,240]{2,1,0:T(8,128)(2,1)}, bf16[4,448,240]{2,1,0:T(8,128)(2,1)}, u32[]{:S(2)}, u32[]{:S(2)}) collective-permute-start(bf16[4,448,240]{2,1,0:T(8,128)(2,1)} %collective-permute-done.19.refs_4_), channel_id=1, source_target_pairs={{0,1},{1,0},{2,3},{3,2},{4,5},{5,4},{6,7},{7,6},{8,9},{9,8},{10,11... | collective-permute-start | bytes 2580488 | tf_op jit(solution)/shard_map/ppermute | solution.py:445
  140.1 25.7 %collective-permute-start.18 = (bf16[4,448,240]{2,1,0:T(8,128)(2,1)}, bf16[4,448,240]{2,1,0:T(8,128)(2,1)}, u32[]{:S(2)}, u32[]{:S(2)}) collective-permute-start(bf16[4,448,240]{2,1,0:T(8,128)(2,1)} %collective-permute-done.17.refs_2_), channel_id=1, source_target_pairs={{0,1},{1,0},{2,3},{3,2},{4,5},{5,4},{6,7},{7,6},{8,9},{9,8},{10,11... | collective-permute-start | bytes 2580488 | tf_op jit(solution)/shard_map/ppermute | solution.py:445
  154.6 11.7 %collective-permute-start.22 = (bf16[4,448,240]{2,1,0:T(8,128)(2,1)}, bf16[4,448,240]{2,1,0:T(8,128)(2,1)}, u32[]{:S(2)}, u32[]{:S(2)}) collective-permute-start(bf16[4,448,240]{2,1,0:T(8,128)(2,1)} %collective-permute-done.21.refs_6_), channel_id=1, source_target_pairs={{0,1},{1,0},{2,3},{3,2},{4,5},{5,4},{6,7},{7,6},{8,9},{9,8},{10,11... | collective-permute-start | bytes 2580488 | tf_op jit(solution)/shard_map/ppermute | solution.py:445
  165.1 14.8 %collective-permute-start.23 = (bf16[4,120,1280]{2,1,0:T(8,128)(2,1)}, bf16[4,120,1280]{2,1,0:T(8,128)(2,1)S(1)}, u32[]{:S(2)}, u32[]{:S(2)}) collective-permute-start(bf16[4,120,1280]{2,1,0:T(8,128)(2,1)} %bitcast_dynamic-update-slice_fusion.refs_0_), channel_id=1, source_target_pairs={{0,1},{1,0},{2,3},{3,2},{4,5},{5,4},{6,7},{7,6},{8,9},{9,8},{10,11... | collective-permute-start | bytes 3686408 | tf_op jit(solution)/shard_map/ppermute | solution.py:445
  165.7 15.3 %collective-permute-start.25 = (bf16[4,120,1280]{2,1,0:T(8,128)(2,1)}, bf16[4,120,1280]{2,1,0:T(8,128)(2,1)S(1)}, u32[]{:S(2)}, u32[]{:S(2)}) collective-permute-start(bf16[4,120,1280]{2,1,0:T(8,128)(2,1)} %collective-permute-done.24.refs_2_), channel_id=1, source_target_pairs={{0,1},{1,0},{2,3},{3,2},{4,5},{5,4},{6,7},{7,6},{8,9},{9,8},{10,11... | collective-permute-start | bytes 3686408 | tf_op jit(solution)/shard_map/ppermute | solution.py:445
  165.8 16.2 %collective-permute-start.27 = (bf16[4,120,1280]{2,1,0:T(8,128)(2,1)}, bf16[4,120,1280]{2,1,0:T(8,128)(2,1)S(1)}, u32[]{:S(2)}, u32[]{:S(2)}) collective-permute-start(bf16[4,120,1280]{2,1,0:T(8,128)(2,1)} %collective-permute-done.26.refs_4_), channel_id=1, source_target_pairs={{0,1},{1,0},{2,3},{3,2},{4,5},{5,4},{6,7},{7,6},{8,9},{9,8},{10,11... | collective-permute-start | bytes 3686408 | tf_op jit(solution)/shard_map/ppermute | solution.py:445
  166.2 16.9 %collective-permute-start.29 = (bf16[4,120,1280]{2,1,0:T(8,128)(2,1)}, bf16[4,120,1280]{2,1,0:T(8,128)(2,1)S(1)}, u32[]{:S(2)}, u32[]{:S(2)}) collective-permute-start(bf16[4,120,1280]{2,1,0:T(8,128)(2,1)} %collective-permute-done.28.refs_6_), channel_id=1, source_target_pairs={{0,1},{1,0},{2,3},{3,2},{4,5},{5,4},{6,7},{7,6},{8,9},{9,8},{10,11... | collective-permute-start | bytes 3686408 | tf_op jit(solution)/shard_map/ppermute | solution.py:445
  276.7 38.9 %collective-permute-start.30 = (bf16[2,960,1280]{2,1,0:T(8,128)(2,1)}, bf16[2,960,1280]{2,1,0:T(8,128)(2,1)}, u32[]{:S(2)}, u32[]{:S(2)}) collective-permute-start(bf16[2,960,1280]{2,1,0:T(8,128)(2,1)} %get-tuple-element.49), channel_id=1, source_target_pairs={{0,1},{1,0},{2,3},{3,2},{4,5},{5,4},{6,7},{7,6},{8,9},{9,8},{10,11... | collective-permute-start | bytes 14745608 | tf_op jit(solution)/shard_map/ppermute | solution.py:445
  288.2 23.5 %collective-permute-start.41 = (bf16[4,448,240]{2,1,0:T(8,128)(2,1)}, bf16[4,448,240]{2,1,0:T(8,128)(2,1)}, u32[]{:S(2)}, u32[]{:S(2)}) collective-permute-start(bf16[4,448,240]{2,1,0:T(8,128)(2,1)} %get-tuple-element.140), channel_id=1, source_target_pairs={{0,2},{2,0},{1,3},{3,1},{4,6},{6,4},{5,7},{7,5},{8,10},{10,8},{9,1... | collective-permute-start | bytes 2580488 | tf_op jit(solution)/shard_map/ppermute | solution.py:445
  299.9 73.9 %collective-permute-start.40 = (bf16[4,448,240]{2,1,0:T(8,128)(2,1)}, bf16[4,448,240]{2,1,0:T(8,128)(2,1)S(1)}, u32[]{:S(2)}, u32[]{:S(2)}) collective-permute-start(bf16[4,448,240]{2,1,0:T(8,128)(2,1)} %get-tuple-element.139), channel_id=1, source_target_pairs={{0,2},{2,0},{1,3},{3,1},{4,6},{6,4},{5,7},{7,5},{8,10},{10,8},{9,1... | collective-permute-start | bytes 2580488 | tf_op jit(solution)/shard_map/ppermute | solution.py:445
  314.0 60.7 %collective-permute-start.42 = (bf16[4,448,240]{2,1,0:T(8,128)(2,1)}, bf16[4,448,240]{2,1,0:T(8,128)(2,1)}, u32[]{:S(2)}, u32[]{:S(2)}) collective-permute-start(bf16[4,448,240]{2,1,0:T(8,128)(2,1)} %fusion.38), channel_id=1, source_target_pairs={{0,4},{4,0},{1,5},{5,1},{2,6},{6,2},{3,7},{7,3},{8,12},{12,8},{9,1... | collective-permute-start | bytes 2580488 | tf_op jit(solution)/shard_map/ppermute | solution.py:445
  319.7 60.2 %collective-permute-start.47 = (bf16[4,120,1280]{2,1,0:T(8,128)(2,1)}, bf16[4,120,1280]{2,1,0:T(8,128)(2,1)}, u32[]{:S(2)}, u32[]{:S(2)}) collective-permute-start(bf16[4,120,1280]{2,1,0:T(8,128)(2,1)} %fusion.33), channel_id=1, source_target_pairs={{0,4},{4,0},{1,5},{5,1},{2,6},{6,2},{3,7},{7,3},{8,12},{12,8},{9,1... | collective-permute-start | bytes 3686408 | tf_op jit(solution)/shard_map/ppermute | solution.py:445
  361.7 22.2 %collective-permute-start.32 = (bf16[2,4,2,120,512]{4,3,2,1,0:T(8,128)(2,1)}, bf16[2,4,2,120,512]{4,3,2,1,0:T(8,128)(2,1)}, u32[]{:S(2)}, u32[]{:S(2)}) collective-permute-start(bf16[2,4,2,120,512]{4,3,2,1,0:T(8,128)(2,1)} %dynamic-slice_bitcast_fusion), channel_id=1, source_target_pairs={{0,1},{1,0},{2,3},{3,2},{4,5},{5,4},{6,7},{7,6},{8,9},{9,8},{10,11... | collective-permute-start | bytes 5898248 | tf_op jit(solution)/shard_map/ppermute | solution.py:445
  372.9 66.9 %collective-permute-start.46 = (bf16[4,120,1280]{2,1,0:T(8,128)(2,1)}, bf16[4,120,1280]{2,1,0:T(8,128)(2,1)}, u32[]{:S(2)}, u32[]{:S(2)}) collective-permute-start(bf16[4,120,1280]{2,1,0:T(8,128)(2,1)} %fusion.29), channel_id=1, source_target_pairs={{0,4},{4,0},{1,5},{5,1},{2,6},{6,2},{3,7},{7,3},{8,12},{12,8},{9,1... | collective-permute-start | bytes 3686408 | tf_op jit(solution)/shard_map/ppermute | solution.py:445
  377.8 11.1 %collective-permute-start.43 = (bf16[448,240]{1,0:T(8,128)(2,1)S(1)}, bf16[448,240]{1,0:T(8,128)(2,1)S(1)}, u32[]{:S(2)}, u32[]{:S(2)}) collective-permute-start(bf16[448,240]{1,0:T(8,128)(2,1)S(1)} %get-tuple-element.169), channel_id=1, source_target_pairs={{0,8},{8,0},{16,24},{24,16},{1,9},{9,1},{17,25},{25,17},{2,10},{10... | collective-permute-start | bytes 645128 | tf_op jit(solution)/shard_map/ppermute | solution.py:449
  377.9 17.8 %collective-permute-start.44 = (bf16[448,240]{1,0:T(8,128)(2,1)S(1)}, bf16[448,240]{1,0:T(8,128)(2,1)S(1)}, u32[]{:S(2)}, u32[]{:S(2)}) collective-permute-start(bf16[448,240]{1,0:T(8,128)(2,1)S(1)} %get-tuple-element.171), channel_id=1, source_target_pairs={{0,16},{8,24},{16,0},{24,8},{1,17},{9,25},{17,1},{25,9},{2,18},{10... | collective-permute-start | bytes 645128 | tf_op jit(solution)/shard_map/ppermute | solution.py:449
  379.9 21.6 %collective-permute-start.45 = (bf16[448,240]{1,0:T(8,128)(2,1)S(1)}, bf16[448,240]{1,0:T(8,128)(2,1)S(1)}, u32[]{:S(2)}, u32[]{:S(2)}) collective-permute-start(bf16[448,240]{1,0:T(8,128)(2,1)S(1)} %get-tuple-element.170), channel_id=1, source_target_pairs={{0,24},{8,16},{16,8},{24,0},{1,25},{9,17},{17,9},{25,1},{2,26},{10... | collective-permute-start | bytes 645128 | tf_op jit(solution)/shard_map/ppermute | solution.py:449
  383.9 55.9 %collective-permute-start.48 = (bf16[4,120,1280]{2,1,0:T(8,128)(2,1)}, bf16[4,120,1280]{2,1,0:T(8,128)(2,1)}, u32[]{:S(2)}, u32[]{:S(2)}) collective-permute-start(bf16[4,120,1280]{2,1,0:T(8,128)(2,1)} %fusion.28), channel_id=1, source_target_pairs={{0,2},{2,0},{1,3},{3,1},{4,6},{6,4},{5,7},{7,5},{8,10},{10,8},{9,1... | collective-permute-start | bytes 3686408 | tf_op jit(solution)/shard_map/ppermute | solution.py:445
  388.9 35.8 %collective-permute-start.34 = (bf16[4,120,512]{2,1,0:T(8,128)(2,1)}, bf16[4,120,512]{2,1,0:T(8,128)(2,1)}, u32[]{:S(2)}, u32[]{:S(2)}) collective-permute-start(bf16[4,120,512]{2,1,0:T(8,128)(2,1)} %get-tuple-element.157), channel_id=1, source_target_pairs={{0,2},{2,0},{1,3},{3,1},{4,6},{6,4},{5,7},{7,5},{8,10},{10,8},{9,1... | collective-permute-start | bytes 1474568 | tf_op jit(solution)/shard_map/ppermute | solution.py:445
  395.7 29.0 %collective-permute-start.35 = (bf16[4,120,512]{2,1,0:T(8,128)(2,1)}, bf16[4,120,512]{2,1,0:T(8,128)(2,1)}, u32[]{:S(2)}, u32[]{:S(2)}) collective-permute-start(bf16[4,120,512]{2,1,0:T(8,128)(2,1)} %get-tuple-element.159), channel_id=1, source_target_pairs={{0,4},{4,0},{1,5},{5,1},{2,6},{6,2},{3,7},{7,3},{8,12},{12,8},{9,1... | collective-permute-start | bytes 1474568 | tf_op jit(solution)/shard_map/ppermute | solution.py:445
  401.5 33.1 %collective-permute-start.36 = (bf16[4,120,512]{2,1,0:T(8,128)(2,1)S(1)}, bf16[4,120,512]{2,1,0:T(8,128)(2,1)}, u32[]{:S(2)}, u32[]{:S(2)}) collective-permute-start(bf16[4,120,512]{2,1,0:T(8,128)(2,1)S(1)} %get-tuple-element.158), channel_id=1, source_target_pairs={{0,6},{2,4},{4,2},{6,0},{1,7},{3,5},{5,3},{7,1},{8,14},{10,12},{12... | collective-permute-start | bytes 1474568 | tf_op jit(solution)/shard_map/ppermute | solution.py:445
  438.5 12.3 %collective-permute-start.39 = (bf16[120,512]{1,0:T(8,128)(2,1)S(1)}, bf16[120,512]{1,0:T(8,128)(2,1)S(1)}, u32[]{:S(2)}, u32[]{:S(2)}) collective-permute-start(bf16[120,512]{1,0:T(8,128)(2,1)S(1)} %get-tuple-element.175), channel_id=1, source_target_pairs={{0,24},{8,16},{16,8},{24,0},{1,25},{9,17},{17,9},{25,1},{2,26},{10... | collective-permute-start | bytes 368648 | tf_op jit(solution)/shard_map/ppermute | solution.py:449
  441.8 13.4 %collective-permute-start.49 = (bf16[120,1280]{1,0:T(8,128)(2,1)S(1)}, bf16[120,1280]{1,0:T(8,128)(2,1)S(1)}, u32[]{:S(2)}, u32[]{:S(2)}) collective-permute-start(bf16[120,1280]{1,0:T(8,128)(2,1)S(1)} %get-tuple-element.166), channel_id=1, source_target_pairs={{0,8},{8,0},{16,24},{24,16},{1,9},{9,1},{17,25},{25,17},{2,10},{10... | collective-permute-start | bytes 921608 | tf_op jit(solution)/shard_map/ppermute | solution.py:449
  444.0 24.6 %collective-permute-start.50 = (bf16[120,1280]{1,0:T(8,128)(2,1)S(1)}, bf16[120,1280]{1,0:T(8,128)(2,1)S(1)}, u32[]{:S(2)}, u32[]{:S(2)}) collective-permute-start(bf16[120,1280]{1,0:T(8,128)(2,1)S(1)} %get-tuple-element.168), channel_id=1, source_target_pairs={{0,16},{8,24},{16,0},{24,8},{1,17},{9,25},{17,1},{25,9},{2,18},{10... | collective-permute-start | bytes 921608 | tf_op jit(solution)/shard_map/ppermute | solution.py:449
  444.1 31.3 %collective-permute-start.51 = (bf16[120,1280]{1,0:T(8,128)(2,1)S(1)}, bf16[120,1280]{1,0:T(8,128)(2,1)S(1)}, u32[]{:S(2)}, u32[]{:S(2)}) collective-permute-start(bf16[120,1280]{1,0:T(8,128)(2,1)S(1)} %get-tuple-element.167), channel_id=1, source_target_pairs={{0,24},{8,16},{16,8},{24,0},{1,25},{9,17},{17,9},{25,1},{2,26},{10... | collective-permute-start | bytes 921608 | tf_op jit(solution)/shard_map/ppermute | solution.py:449
  (69 other events, 738.2 us)
